TPU v7x, 256 devices: a whole 4x4x8 slice. The times are simulated.
256 devices in a mesh: gx: 16 (over x, y), gy: 16 (over z, core).
Axes of the slice: x: 4, y: 4, z: 8, core: 2. Of those that a mesh axis runs over, the one named last changes fastest.
Arguments:
- raw_basis: float32 [512, 256, 4, 128], P('gx', 'gy'), may hold values from -600 to 600, as said below
- coefficients: float32 [4, 512, 256, 4], P(None, 'gx', 'gy'), may hold values from 0.25 to 4
- nominal_weights: float32 [4], replicated, may hold values from 0.5 to 2
Outputs:
- ortho_basis: float32 [512, 256, 4, 128], P('gx', 'gy')
- nominal_image: float32 [512, 256, 4, 128], P('gx', 'gy')
- reduced_ops: float32 [4, 128, 128], replicated
- residual_grams: float32 [10, 128, 128], replicated
Inputs may be any that keep to these rules, and one draw needn't show every extreme that they name: `raw_basis`: the columns are linearly independent.
All inputs are finite; a program needn't handle non-finite values.
Results may differ from a plain program's by a relative error of at most 0.0001.
Values sent between devices are 32-bit elements; how exact they have to be, the bound alone decides.
No kernel may reach another device: no remote copies, remote signals or barrier semaphores. Data moves between devices by JAX's collectives and lax.ppermute only.
A program may use at most 64 MiB of HBM per device.

v0:
```python
import jax
import jax.numpy as jnp
from jax import lax
from jax.sharding import PartitionSpec as P

directions = ((1, 0, 0), (-1, 0, 0), (0, 1, 0), (0, -1, 0), (0, 0, 1), (0, 0, -1))
operator_pairs = ((0, 0), (0, 1), (0, 2), (0, 3), (1, 1), (1, 2), (1, 3), (2, 2), (2, 3), (3, 3))


def extended(cells, sides, width):
    for axis, dim in sides:
        count = lax.axis_size(axis)
        ends = count - 1
        head = lax.slice_in_dim(cells, 0, width, axis=dim)
        tail = lax.slice_in_dim(cells, cells.shape[dim] - width, cells.shape[dim], axis=dim)
        cells = jnp.concatenate(
            [
                lax.ppermute(tail, axis, [(i, (i + 1) % count) for i in range(ends)]),
                cells,
                lax.ppermute(head, axis, [((i + 1) % count, i) for i in range(ends)]),
            ],
            axis=dim,
        )
    return cells


def window(values, leading, along_x, along_y, along_z):
    selector = [slice(None)] * values.ndim
    for position, offset in zip(range(leading, leading + 3), (along_x, along_y, along_z)):
        selector[position] = slice(1 + offset, values.shape[position] - 1 + offset)
    return values[tuple(selector)]


def apply_all(padded_basis, padded_coef):
    centre = window(padded_basis, 0, 0, 0, 0)
    centre_coef = window(padded_coef, 1, 0, 0, 0)
    images = [jnp.zeros_like(centre) for member in range(4)]
    for direction in directions:
        differ = centre - window(padded_basis, 0, *direction)
        weights = 0.5 * (centre_coef + window(padded_coef, 1, *direction))
        images = [images[member] + weights[member][..., None] * differ for member in range(4)]
    return jnp.stack(images)


def weighted(nominal_weights, images):
    total = nominal_weights[0] * images[0]
    for member in range(1, 4):
        total = total + nominal_weights[member] * images[member]
    return total


def inverse_factor(gram):
    factor = jnp.linalg.cholesky(gram)
    return jax.scipy.linalg.solve_triangular(
        factor, jnp.eye(gram.shape[0], dtype=gram.dtype), lower=True
    )


def local_grams(left_flat, image_flat):
    reduced = jnp.einsum("cr,kcs->krs", left_flat, image_flat, precision=lax.Precision.HIGHEST)
    crossed = jnp.stack(
        [
            jnp.einsum(
                "cr,cs->rs",
                image_flat[first_op],
                image_flat[second_op],
                precision=lax.Precision.HIGHEST,
            )
            for first_op, second_op in operator_pairs
        ]
    )
    return (reduced, crossed)


def shards(raw_basis, coefficients, nominal_weights):
    width = raw_basis.shape[3]
    total_cells = (
        raw_basis.shape[0]
        * raw_basis.shape[1]
        * raw_basis.shape[2]
        * lax.axis_size("gx")
        * lax.axis_size("gy")
    )
    coef_halo = extended(coefficients, (("gx", 1), ("gy", 2)), 1)
    padded_coef = jnp.pad(coef_halo, ((0, 0), (0, 0), (0, 0), (1, 1)))
    flat = raw_basis.reshape(-1, width)
    gram_local = jnp.einsum("cr,cs->rs", flat, flat, precision=lax.Precision.HIGHEST)
    gram = lax.psum(gram_local, ("gx", "gy")) / total_cells
    inverse = inverse_factor(gram)
    ortho_flat = jnp.dot(flat, inverse.T, precision=lax.Precision.HIGHEST)
    ortho_basis = ortho_flat.reshape(raw_basis.shape)
    basis_halo = extended(ortho_basis, (("gx", 0), ("gy", 1)), 1)
    images = apply_all(jnp.pad(basis_halo, ((0, 0), (0, 0), (1, 1), (0, 0))), padded_coef)
    reduced, crossed = local_grams(ortho_flat, images.reshape(4, -1, width))
    reduced_sum, crossed_sum = lax.psum((reduced, crossed), ("gx", "gy"))
    reduced_ops = reduced_sum / total_cells
    residual_grams = crossed_sum / total_cells
    nominal_image = weighted(nominal_weights, images)
    return (ortho_basis, nominal_image, reduced_ops, residual_grams)


def solution(mesh):
    in_specs = (P("gx", "gy", None, None), P(None, "gx", "gy", None), P())
    out_specs = (P("gx", "gy", None, None), P("gx", "gy", None, None), P(), P())
    return jax.shard_map(shards, mesh=mesh, in_specs=in_specs, out_specs=out_specs, check_vma=False)
```

profile of v0, /device:TPU:1, one launch (start us, length us, event | category | flops | bytes accessed | tf_op | source)
XLA Modules:
  0.0 657.4 jit_solution(11169612522300881029)
XLA Ops:
  8.4 4.0 collective-permute-start.2
  13.8 5.0 convolution_bitcast_fusion.10
  19.8 4.8 collective-permute-start.6
  24.6 2.2 collective-permute-start.4
  31.4 233.7 %all-reduce.6.cloned.1.call-done = f32[128,128]{0,1:T(8,128)} async-done(((f32[128,128]{0,1:T(8,128)}), f32[128,128]{0,1:T(8,128)}) %all-reduce.6.cloned.1.call-update) | async-done | bytes 65552 | tf_op jit(solution)/shard_map/psum | solution.py:88
  266.9 11.7 %cholesky.17 = f32[128,128]{1,0:T(8,128)S(1)} custom-call(f32[128,128]{1,0:T(8,128)S(1)} %fusion.58), custom_call_target="Cholesky" | custom-call | tf_op jit(solution)/shard_map/jit(cholesky)/cholesky | solution.py:53
  279.9 9.8 %custom-call.7 = f32[1,128,128]{1,2,0:T(8,128)S(1)} custom-call(f32[1,128,128]{2,1,0:T(8,128)S(1)} %fusion.55), custom_call_target="InvertDiagBlocksLowerTriangular" | custom-call | tf_op jit(solution)/shard_map/jit(_solve_triangular)/triangular_solve | solution.py:54
  292.6 4.0 collective-permute-start.3
  298.3 3.5 collective-permute-start.7
  301.7 2.4 collective-permute-start.5
  328.7 18.0 %multiply_add_fusion = (f32[32,16,4,128]{3,2,1,0:T(4,128)}, f32[32,16,4,128]{3,2,1,0:T(4,128)S(1)}, f32[32,16,4,128]{3,2,1,0:T(4,128)S(1)}, f32[32,16,4,128]{3,2,1,0:T(4,128)S(1)}, f32[32,16,4,128]{3,2,1,0:T(4,128)S(1)}) fusion(f32[]{:T(128)} %bitcast.30, f32[]{:T(128)} %bitcast.23, f32[]{:T(128)} %bitcast.16, f32[]{:T(128)} %bitcast.7, ...), kind=kLoop, calls=%fused_computation.53 | loop fusion | flops 16515072 | bytes 8790032 | tf_op jit(solution)/shard_map/add | solution.py:48
  346.7 2.8 fusion.21
  349.5 2.8 fusion.20
  352.3 2.8 fusion.19
  355.1 2.8 fusion.18
  357.9 3.0 fusion.17
  360.9 2.8 fusion.16
  363.7 2.8 fusion.15
  366.5 2.8 fusion.14
  369.3 3.1 fusion.13
  372.4 2.8 fusion.12
  376.0 2.5 copy.106
  381.6 6.0 fusion.9
  387.6 258.8 %all-reduce.8.cloned.1.call-done = (f32[4,128,128]{1,2,0:T(8,128)}, f32[10,128,128]{2,1,0:T(8,128)}) async-done(((f32[4,128,128]{1,2,0:T(8,128)}, f32[10,128,128]{2,1,0:T(8,128)}), (f32[4,128,128]{1,2,0:T(8,128)}, f32[10,128,128]{2,1,0:T(8,128)})) %all-reduce.8.cloned.1.call-update) | async-done | bytes 917520 | tf_op jit(solution)/shard_map/psum | solution.py:95
  (139 shorter events, 47.4 us)
Async XLA Ops:
  7.2 23.5 %copy-start.7 = (f32[4,32,16,4]{1,3,2,0:T(4,128)S(1)}, f32[4,32,16,4]{1,3,2,0:T(4,128)}, u32[]{:S(2)}) copy-start(f32[4,32,16,4]{1,3,2,0:T(4,128)} %param.4) | copy-start | bytes 98308
  7.2 257.9 %all-reduce.6.cloned.1.call-start = ((), (), s32[]{:S(2)}) async-start(), calls=%async_computation | async-start | bytes 131072 | tf_op jit(solution)/shard_map/psum | solution.py:88
  8.4 10.6 %collective-permute-start.2 = (f32[4,1,16,4]{1,3,2,0:T(4,128)S(1)}, f32[4,1,16,4]{1,3,2,0:T(4,128)S(1)}, u32[]{:S(2)}, u32[]{:S(2)}) collective-permute-start(f32[4,1,16,4]{1,3,2,0:T(4,128)S(1)} %get-tuple-element.59), channel_id=1, source_target_pairs={{0,16},{16,32},{32,48},{48,64},{64,80},{80,96},{96,112},{112,128},... | collective-permute-start | bytes 3080 | tf_op jit(solution)/shard_map/ppermute | solution.py:18
  12.4 277.6 %copy-start.6 = (f32[32,16,4,128]{3,2,1,0:T(4,128)S(1)}, f32[32,16,4,128]{3,2,1,0:T(4,128)}, u32[]{:S(2)}) copy-start(f32[32,16,4,128]{3,2,1,0:T(4,128)} %param.3) | copy-start | bytes 3145732
  12.4 6.5 collective-permute-start
  18.9 627.4 %all-reduce.8.cloned.1.call-start = ((), (), s32[]{:S(2)}) async-start(), calls=%async_computation.1 | async-start | bytes 1835008 | tf_op jit(solution)/shard_map/psum | solution.py:95
  19.8 8.5 %collective-permute-start.6 = (f32[4,34,1,4]{1,3,2,0:T(4,128)S(1)}, f32[4,34,1,4]{1,3,2,0:T(4,128)S(1)}, u32[]{:S(2)}, u32[]{:S(2)}) collective-permute-start(f32[4,34,1,4]{1,3,2,0:T(4,128)S(1)} %get-tuple-element.29), channel_id=1, source_target_pairs={{0,1},{1,2},{2,3},{3,4},{4,5},{5,6},{6,7},{7,8},{8,9},{9,10},{10,1... | collective-permute-start | bytes 6536 | tf_op jit(solution)/shard_map/ppermute | solution.py:18
  24.6 5.0 collective-permute-start.4
  291.0 14.0 %copy-start.4 = (f32[128,2048]{1,0:T(8,128)}, f32[128,2048]{1,0:T(8,128)S(1)}, u32[]{:S(2)}) copy-start(f32[128,2048]{1,0:T(8,128)S(1)} %fusion.63) | copy-start | bytes 3145732
  291.3 5.7 collective-permute-start.1
  292.6 5.0 collective-permute-start.3
  296.9 30.0 %copy-start = (f32[2048,128]{1,0:T(8,128)}, f32[2048,128]{1,0:T(8,128)S(1)}, u32[]{:S(2)}) copy-start(f32[2048,128]{1,0:T(8,128)S(1)} %copy.76) | copy-start | bytes 3145732
  298.3 27.2 %collective-permute-start.7 = (f32[34,1,4,128]{3,2,1,0:T(4,128)}, f32[34,1,4,128]{3,2,1,0:T(4,128)S(1)}, u32[]{:S(2)}, u32[]{:S(2)}) collective-permute-start(f32[34,1,4,128]{3,2,1,0:T(4,128)} %get-tuple-element.21), channel_id=1, source_target_pairs={{0,1},{1,2},{2,3},{3,4},{4,5},{5,6},{6,7},{7,8},{8,9},{9,10},{10,1... | collective-permute-start | bytes 208904 | tf_op jit(solution)/shard_map/ppermute | solution.py:18
  301.7 23.7 %collective-permute-start.5 = (f32[34,1,4,128]{3,2,1,0:T(4,128)}, f32[34,1,4,128]{3,2,1,0:T(4,128)S(1)}, u32[]{:S(2)}, u32[]{:S(2)}) collective-permute-start(f32[34,1,4,128]{3,2,1,0:T(4,128)} %get-tuple-element.22), channel_id=1, source_target_pairs={{1,0},{2,1},{3,2},{4,3},{5,4},{6,5},{7,6},{8,7},{9,8},{10,9},{11,1... | collective-permute-start | bytes 208904 | tf_op jit(solution)/shard_map/ppermute | solution.py:20
  304.8 13.6 %copy-start.35 = (f32[32,16,4]{0,2,1:T(4,128)S(1)}, f32[32,16,4]{0,2,1:T(4,128)}, u32[]{:S(2)}) copy-start(f32[32,16,4]{0,2,1:T(4,128)} %get-tuple-element.55) | copy-start | bytes 24580
  304.8 14.4 %copy-start.34 = (f32[32,16,4]{0,2,1:T(4,128)S(1)}, f32[32,16,4]{0,2,1:T(4,128)}, u32[]{:S(2)}) copy-start(f32[32,16,4]{0,2,1:T(4,128)} %get-tuple-element.56) | copy-start | bytes 24580
  305.0 15.1 %copy-start.33 = (f32[32,16,4]{0,2,1:T(4,128)S(1)}, f32[32,16,4]{0,2,1:T(4,128)}, u32[]{:S(2)}) copy-start(f32[32,16,4]{0,2,1:T(4,128)} %get-tuple-element.57) | copy-start | bytes 24580
  326.3 2.1 copy-start.24
  326.3 2.2 copy-start.25
  326.3 2.3 copy-start.26
  326.4 2.3 copy-start.27
  346.7 22.6 %copy-start.1 = (f32[32,16,4,128]{3,2,1,0:T(4,128)}, f32[32,16,4,128]{3,2,1,0:T(4,128)S(1)}, u32[]{:S(2)}) copy-start(f32[32,16,4,128]{3,2,1,0:T(4,128)S(1)} %get-tuple-element.17) | copy-start | bytes 3145732
  346.7 25.7 %copy-start.3 = (f32[32,16,4,128]{3,2,1,0:T(4,128)}, f32[32,16,4,128]{3,2,1,0:T(4,128)S(1)}, u32[]{:S(2)}) copy-start(f32[32,16,4,128]{3,2,1,0:T(4,128)S(1)} %get-tuple-element.18) | copy-start | bytes 3145732
  372.4 6.2 copy-start.2
  (22 other events, 32.9 us)
Sparse Core Ops, SparseCore 0:
  19.0 246.0 all-reduce.5
  387.7 258.5 all-reduce.7
where the time goes:
time: 661 us; the launch traced here: 657 us
  waiting for transfers between devices  494 us (75%)
  other arithmetic  50 us (8%)
  matrix products  40.7 us (6%)
  local copies, waits for them, and re-layouts  33.5 us (5%)
  starting transfers between devices  23.8 us (4%)
  between operations  15.1 us (2%)
    psum x1, waiting for transfers between devices, shards(): reduced_sum, crossed_sum = lax.psum((reduced, crossed), ('gx', 'gy'))  259 us
    psum x1, waiting for transfers between devices, shards(): gram = lax.psum(gram_local, ('gx', 'gy')) / total_cells  234 us
    dot_general x10, matrix products, local_grams(): jnp.einsum('cr,cs->rs', image_flat[first_op], image_flat[second_op], prec...  28.5 us
    mul x27, local copies, waits for them, and re-layouts, apply_all(): weights[member][..., None] * differ  21.3 us
    add x1, other arithmetic, weighted(): total = total + nominal_weights[member] * images[member]  18 us
    ppermute x4, starting transfers between devices, extended(): lax.ppermute(tail, axis, [(i, (i + 1) % count) for i in range(ends)])  16.3 us
  transfers between devices with their start and end apart: 10, of which 4 were waited for; matrix products, arithmetic and copies ran while one was open for 5% of the time, Pallas kernels for 0%

commit v1 on v0

v1 whole, which is shorter than its diff:
```python
import jax
import jax.numpy as jnp
from jax import lax
from jax.experimental import pallas as pl
from jax.experimental.pallas import tpu as pltpu
from jax.sharding import PartitionSpec as P

R = 128
TERMS = 4
operator_pairs = ((0, 0), (0, 1), (0, 2), (0, 3), (1, 1), (1, 2), (1, 3), (2, 2), (2, 3), (3, 3))
crossed_pairs = tuple(pair for pair in operator_pairs if pair[0] != pair[1])
HIGHEST = lax.Precision.HIGHEST
f32, bf16 = jnp.float32, jnp.bfloat16

SLOTS = 12
HALF = SLOTS // 2 * R
SLAB = 64
CHUNK = 4


def faces_kernel(basis, coef, x_low, x_high, y_low, y_high):
    lane = lax.broadcasted_iota(jnp.int32, (SLAB, R), 1)
    slabs = basis.shape[0] // SLAB
    x_low[0:SLAB, :] = basis[0:SLAB, :]
    x_high[0:SLAB, :] = basis[(slabs - 1) * SLAB : slabs * SLAB, :]
    low = jnp.zeros((SLAB, R), f32)
    high = jnp.zeros((SLAB, R), f32)
    for k in range(TERMS):
        rows = coef[k * SLAB : (k + 1) * SLAB, :]
        low = jnp.where(lane == k, rows[:, 0:1], low)
        high = jnp.where(lane == k, rows[:, slabs - 1 : slabs], high)
    x_low[SLAB : 2 * SLAB, :] = low
    x_high[SLAB : 2 * SLAB, :] = high
    for x in range(slabs):
        y_low[4 * x : 4 * x + 4, :] = basis[x * SLAB : x * SLAB + 4, :]
        y_high[4 * x : 4 * x + 4, :] = basis[x * SLAB + SLAB - 4 : (x + 1) * SLAB, :]
    y_low[4 * slabs :, :] = jnp.zeros((16, R), f32)
    y_high[4 * slabs :, :] = jnp.zeros((16, R), f32)
    for k in range(TERMS):
        y_low[4 * (slabs + k) : 4 * (slabs + k) + 4, 0:slabs] = coef[k * SLAB : k * SLAB + 4, :]
        y_high[4 * (slabs + k) : 4 * (slabs + k) + 4, 0:slabs] = coef[(k + 1) * SLAB - 4 : (k + 1) * SLAB, :]


def images_kernel(
    me, weights, basis, coef, from_left, from_right, from_below, from_above, mine, other, nominal,
    extended, face, top, bottom, product, packed,
):
    slabs = basis.shape[0] // SLAB
    extended[0:SLAB, :] = from_left[0:SLAB, :]
    extended[SLAB : (slabs + 1) * SLAB, :] = basis[...]
    extended[(slabs + 1) * SLAB :, :] = from_right[0:SLAB, :]
    product[...] = jnp.zeros_like(product)

    row = lax.broadcasted_iota(jnp.int32, (SLAB, R), 0)
    lane = lax.broadcasted_iota(jnp.int32, (SLAB, R), 1)
    level = row % 4
    row8 = lax.broadcasted_iota(jnp.int32, (8, R), 0)

    for k in range(TERMS):
        own = jnp.concatenate([coef[k * SLAB : (k + 1) * SLAB, :], jnp.zeros((SLAB, R - slabs), f32)], axis=1)
        right = jnp.where(lane == slabs, from_right[SLAB : 2 * SLAB, k : k + 1], own)
        left = jnp.where(lane == 0, from_left[SLAB : 2 * SLAB, k : k + 1], pltpu.roll(own, 1, 1))
        face[k, 0] = 0.5 * (left + right)
        pair = 4 * slabs + 8 * (k // 2)
        above = from_above[pair : pair + 8, :]
        below = from_below[pair : pair + 8, :]
        if k % 2 == 0:
            above = pltpu.roll(above, 4, 0)
        else:
            below = pltpu.roll(below, 4, 0)
        up = pltpu.roll(own, SLAB - 4, 0)
        up = jnp.concatenate([up[: SLAB - 8], jnp.where(row8 >= 4, above, up[SLAB - 8 :])], axis=0)
        down = pltpu.roll(own, 4, 0)
        down = jnp.concatenate([jnp.where(row8 < 4, below, down[:8]), down[8:]], axis=0)
        face[k, 1] = 0.5 * (own + up)
        face[k, 2] = 0.5 * (own + down)
        face[k, 3] = 0.5 * (own + jnp.where(level < 3, pltpu.roll(own, SLAB - 1, 0), 0.0))
        face[k, 4] = 0.5 * (own + jnp.where(level > 0, pltpu.roll(own, 1, 0), 0.0))

    def chunk(c, carry):
        shift = lax.rem(R - c * CHUNK, R)
        moved = [[pltpu.roll(face[k, f], shift, 1) for f in range(5)] for k in range(TERMS)]
        for s in range(CHUNK):
            x = c * CHUNK + s
            base = pl.multiple_of(x * SLAB, SLAB)
            v = extended[pl.ds(pl.multiple_of(base + SLAB, SLAB), SLAB), :]
            pair = pl.multiple_of((c * (CHUNK // 2) + s // 2) * 8, 8)
            above = from_above[pl.ds(pair, 8), :]
            below = from_below[pl.ds(pair, 8), :]
            if s % 2 == 0:
                above = pltpu.roll(above, 4, 0)
            else:
                below = pltpu.roll(below, 4, 0)
            up = pltpu.roll(v, SLAB - 4, 0)
            up = jnp.concatenate([up[: SLAB - 8], jnp.where(row8 >= 4, above, up[SLAB - 8 :])], axis=0)
            down = pltpu.roll(v, 4, 0)
            down = jnp.concatenate([jnp.where(row8 < 4, below, down[:8]), down[8:]], axis=0)
            steps = (
                v - extended[pl.ds(base, SLAB), :],
                v - extended[pl.ds(pl.multiple_of(base + 2 * SLAB, SLAB), SLAB), :],
                v - up,
                v - down,
                v - jnp.where(level < 3, pltpu.roll(v, SLAB - 1, 0), 0.0),
                v - jnp.where(level > 0, pltpu.roll(v, 1, 0), 0.0),
            )
            total = jnp.zeros((SLAB, R), f32)
            for block in range(TERMS + 1):
                if block == 0:
                    value = v
                else:
                    k = block - 1
                    columns = [moved[k][0][:, s : s + 1], moved[k][0][:, s + 1 : s + 2]]
                    columns += [moved[k][f][:, s : s + 1] for f in range(1, 5)]
                    value = columns[0] * steps[0]
                    for column, step in zip(columns[1:], steps[1:]):
                        value = value + column * step
                    total = total + weights[k] * value
                high = value.astype(bf16)
                low = (value - high.astype(f32)).astype(bf16)
                top[s * SLAB : (s + 1) * SLAB, block * R : (block + 1) * R] = high
                bottom[s * SLAB : (s + 1) * SLAB, block * R : (block + 1) * R] = low
            nominal[pl.ds(base, SLAB), :] = total
        turned = top[...].T
        width = (TERMS + 1) * R
        for start in range(0, 2 * width, 256):
            rows = min(start + 256, width)
            if start + 256 <= width:
                right = top[:, start : start + 256]
            elif start < width:
                right = jnp.concatenate([top[:, start:width], bottom[:, 0 : start + 256 - width]], axis=1)
            else:
                right = bottom[:, start - width : start + 256 - width]
            product[0:rows, start : start + 256] += jnp.dot(turned[0:rows], right, preferred_element_type=f32)
        return carry

    lax.fori_loop(0, slabs // CHUNK, chunk, 0)

    width = (TERMS + 1) * R

    def gram(a, b):
        high = product[a * R : (a + 1) * R, b * R : (b + 1) * R]
        first = product[a * R : (a + 1) * R, width + b * R : width + (b + 1) * R]
        second = product[b * R : (b + 1) * R, width + a * R : width + (a + 1) * R]
        return high + first + second.T

    r = lax.broadcasted_iota(jnp.int32, (R, R), 0)
    c = lax.broadcasted_iota(jnp.int32, (R, R), 1)
    packed[0:R, :] = gram(0, 0)
    symmetric = [(0, k + 1) for k in range(TERMS)] + [(k + 1, k + 1) for k in range(TERMS)]
    packed[(SLOTS - 1) * R :, :] = jnp.zeros((R, R), f32)
    for p in range(4):
        one, two = gram(*symmetric[2 * p]), gram(*symmetric[2 * p + 1])
        packed[(p + 1) * R : (p + 2) * R, :] = jnp.where(c >= r, one, two)
        packed[(SLOTS - 1) * R + p : (SLOTS - 1) * R + p + 1, :] = jnp.sum(
            jnp.where(c == r, two, 0.0), axis=0, keepdims=True
        )
    for q, (a, b) in enumerate(crossed_pairs):
        packed[(q + 5) * R : (q + 6) * R, :] = gram(a + 1, b + 1)
    mine[...] = packed[pl.ds(pl.multiple_of(me[0] * HALF, R), HALF), :]
    other[...] = packed[pl.ds(pl.multiple_of((1 - me[0]) * HALF, R), HALF), :]


def finish_kernel(me, mine, other, basis, nominal, ortho_out, nominal_out, reduced_out, residual_out, packed, inverse, *, cells):
    packed[pl.ds(pl.multiple_of(me[0] * HALF, R), HALF), :] = mine[...]
    packed[pl.ds(pl.multiple_of((1 - me[0]) * HALF, R), HALF), :] = other[...]
    scale = 1.0 / cells
    row8 = lax.broadcasted_iota(jnp.int32, (8, R), 0)
    lane8 = lax.broadcasted_iota(jnp.int32, (8, R), 1)
    blocks = R // 8
    left = [packed[8 * i : 8 * i + 8, :] * scale for i in range(blocks)]
    right = [jnp.where(row8 + 8 * i == lane8, 1.0, 0.0).astype(f32) for i in range(blocks)]
    for j in range(R):
        i0, r0 = divmod(j, 8)
        pivot_row = left[i0][r0 : r0 + 1, :]
        right_row = right[i0][r0 : r0 + 1, :]
        pivot = pivot_row[:, j : j + 1]
        inverse[j : j + 1, :] = right_row * (1.0 / jnp.sqrt(pivot))
        scaled_left = pivot_row * (1.0 / pivot)
        scaled_right = right_row * (1.0 / pivot)
        for i in range(i0, blocks):
            column = left[i][:, j : j + 1]
            if i == i0:
                if r0 == 7:
                    continue
                column = jnp.where(row8 > r0, column, 0.0)
            left[i] = left[i] - column * scaled_left
            right[i] = right[i] - column * scaled_right
    inv = inverse[...]
    inv_t = inv.T
    ortho_out[...] = jnp.dot(basis[...], inv_t, precision=HIGHEST, preferred_element_type=f32)
    nominal_out[...] = jnp.dot(nominal[...], inv_t, precision=HIGHEST, preferred_element_type=f32)

    r = lax.broadcasted_iota(jnp.int32, (R, R), 0)
    c = lax.broadcasted_iota(jnp.int32, (R, R), 1)

    def moved(matrix):
        half = jnp.dot(matrix * scale, inv_t, precision=HIGHEST, preferred_element_type=f32)
        return jnp.dot(inv, half, precision=HIGHEST, preferred_element_type=f32)

    for p in range(4):
        pair = packed[(p + 1) * R : (p + 2) * R, :]
        turned = pair.T
        diagonal = packed[(SLOTS - 1) * R + p : (SLOTS - 1) * R + p + 1, :]
        one = moved(jnp.where(c >= r, pair, turned))
        two = moved(jnp.where(c < r, pair, jnp.where(c == r, diagonal, turned)))
        if p < 2:
            reduced_out[2 * p] = one
            reduced_out[2 * p + 1] = two
        else:
            k = 2 * (p - 2)
            residual_out[operator_pairs.index((k, k))] = one
            residual_out[operator_pairs.index((k + 1, k + 1))] = two
    for q, (a, b) in enumerate(crossed_pairs):
        residual_out[operator_pairs.index((a, b))] = moved(packed[(q + 5) * R : (q + 6) * R, :])


def summed(values, half, groups):
    count = lax.axis_size("gx")
    width = values.shape[1]
    parts = values.reshape(count, -1, width)
    shard = jnp.sum(lax.all_to_all(parts, "gx", 0, 0), axis=0)
    depth = len(groups[0])
    along = jnp.broadcast_to(shard[None], (depth,) + shard.shape)
    shard = jnp.sum(lax.all_to_all(along, "gy", 0, 0, axis_index_groups=groups), axis=0)
    spread = jnp.broadcast_to(shard[None], (count,) + shard.shape)
    return lax.all_to_all(spread, "gx", 0, 0).reshape(values.shape)


def shards(raw_basis, coefficients, nominal_weights):
    nx, ny, nz, width = raw_basis.shape
    count_x, count_y = lax.axis_size("gx"), lax.axis_size("gy")
    cells = nx * ny * nz * count_x * count_y
    flat = raw_basis.reshape(-1, width)
    coef = jnp.transpose(coefficients, (0, 2, 3, 1)).reshape(-1, nx)
    vmem = pl.BlockSpec(memory_space=pltpu.VMEM)
    smem = pl.BlockSpec(memory_space=pltpu.SMEM)

    def array(*shape):
        return jax.ShapeDtypeStruct(shape, f32)

    y_rows = 4 * nx + 4 * TERMS
    x_low, x_high, y_low, y_high = pl.pallas_call(
        faces_kernel,
        out_shape=(array(2 * SLAB, R), array(2 * SLAB, R), array(y_rows, R), array(y_rows, R)),
        in_specs=[vmem, vmem],
        out_specs=(vmem,) * 4,
        name="faces",
    )(flat, coef)
    up_x = [(i, i + 1) for i in range(count_x - 1)]
    up_y = [(i, i + 1) for i in range(count_y - 1)]
    from_left = lax.ppermute(x_high, "gx", up_x)
    from_right = lax.ppermute(x_low, "gx", [(b, a) for a, b in up_x])
    from_below = lax.ppermute(y_high, "gy", up_y)
    from_above = lax.ppermute(y_low, "gy", [(b, a) for a, b in up_y])

    me = (lax.axis_index("gy") % 2).astype(jnp.int32).reshape(1)
    mine, other, raw_nominal = pl.pallas_call(
        images_kernel,
        out_shape=(array(HALF, R), array(HALF, R), array(nx * SLAB, R)),
        in_specs=[smem, smem] + [vmem] * 6,
        out_specs=(vmem,) * 3,
        scratch_shapes=[
            pltpu.VMEM(((nx + 2) * SLAB, R), f32),
            pltpu.VMEM((TERMS, 5, SLAB, R), f32),
            pltpu.VMEM((CHUNK * SLAB, (TERMS + 1) * R), bf16),
            pltpu.VMEM((CHUNK * SLAB, (TERMS + 1) * R), bf16),
            pltpu.VMEM(((TERMS + 1) * R, 2 * (TERMS + 1) * R), f32),
            pltpu.VMEM((SLOTS * R, R), f32),
        ],
        name="images",
    )(me, nominal_weights, flat, coef, from_left, from_right, from_below, from_above)

    swap = [(i, i ^ 1) for i in range(count_y)]
    groups = [list(range(core, count_y, 2)) for core in range(2)]
    mine = mine + lax.ppermute(other, "gy", swap)
    mine = summed(mine, HALF, groups)
    other = lax.ppermute(mine, "gy", swap)

    def finish(*refs):
        finish_kernel(*refs, cells=cells)

    ortho, nominal, reduced_ops, residual_grams = pl.pallas_call(
        finish,
        out_shape=(array(nx * SLAB, R), array(nx * SLAB, R), array(TERMS, R, R), array(len(operator_pairs), R, R)),
        in_specs=[smem] + [vmem] * 4,
        out_specs=(vmem,) * 4,
        scratch_shapes=[pltpu.VMEM((SLOTS * R, R), f32), pltpu.VMEM((R, R), f32)],
        name="finish",
    )(me, mine, other, flat, raw_nominal)
    shape = raw_basis.shape
    return (ortho.reshape(shape), nominal.reshape(shape), reduced_ops, residual_grams)


def solution(mesh):
    in_specs = (P("gx", "gy", None, None), P(None, "gx", "gy", None), P())
    out_specs = (P("gx", "gy", None, None), P("gx", "gy", None, None), P(), P())
    return jax.shard_map(shards, mesh=mesh, in_specs=in_specs, out_specs=out_specs, check_vma=False)
```

time: 661 us -> 113 us (0.17)
  waiting for transfers between devices: 494 us -> 7.19 us
  other arithmetic: 50 us -> 1.1 us
  blocking collectives: 0 us -> 47.5 us
  matrix products: 40.7 us -> 0 us
  Pallas kernels: 0 us -> 39.5 us
  local copies, waits for them, and re-layouts: 33.5 us -> 1.44 us
  between operations: 15.1 us -> 0.73 us
  starting transfers between devices: 23.8 us -> 15.5 us
    psum x2 -> x0, waiting for transfers between devices: 492 us -> none  [the longest x1 259 us: shards(): reduced_sum, crossed_sum = lax.psum((reduced, crossed), ('gx', 'gy'))]
    all_to_all x0 -> x3, blocking collectives: none -> 47.5 us  [the longest x1 19.2 us: summed(): lax.all_to_all(along, 'gy', 0, 0, axis_index_groups=groups)]
    dot_general x13 -> x0, matrix products: 40.5 us -> none  [the longest x10 28.5 us: local_grams(): jnp.einsum('cr,cs->rs', image_flat[first_op], image_flat[second_op], prec...]
    pallas_call x0 -> x3, Pallas kernels: none -> 39.5 us  [the longest x1 21.2 us: shards(): pl.pallas_call(finish, out_shape=(array(nx * SLAB, R), array(nx * SLAB, R...]
    another operation x5 -> x0, other arithmetic: 22.9 us -> none  [the longest x3 12.4 us: inverse_factor(): factor = jnp.linalg.cholesky(gram)]
    mul x27 -> x0, local copies, waits for them, and re-layouts: 21.3 us -> none  [apply_all(): weights[member][..., None] * differ]
    add x1, other arithmetic: 18 us -> 1.05 us  [shards(): mine = mine + lax.ppermute(other, 'gy', swap)]
    ppermute x8 -> x6, starting transfers between devices: 23.7 us -> 15.5 us  [the longest x1 4.91 us: shards(): from_below = lax.ppermute(y_high, 'gy', up_y)]
  transfers between devices with their start and end apart: 10 -> 6, of which waited for: 4 -> 4; matrix products, arithmetic and copies ran while one was open for 5% -> 0% of each run, Pallas kernels for 0% -> 0%
where the time goes in v1:
time: 113 us
  blocking collectives  47.5 us (42%)
  Pallas kernels  39.5 us (35%)
  starting transfers between devices  15.5 us (14%)
  waiting for transfers between devices  7.19 us (6%)
  local copies, waits for them, and re-layouts  1.44 us (1%)
    pallas_call x1, Pallas kernels, shards(): pl.pallas_call(finish, out_shape=(array(nx * SLAB, R), array(nx * SLAB, R...  21.2 us
    all_to_all x1, blocking collectives, summed(): lax.all_to_all(along, 'gy', 0, 0, axis_index_groups=groups)  19.2 us
    all_to_all x1, blocking collectives, summed(): shard = jnp.sum(lax.all_to_all(parts, 'gx', 0, 0), axis=0)  17 us
    pallas_call x1, Pallas kernels, shards(): pl.pallas_call(images_kernel, out_shape=(array(HALF, R), array(HALF, R),...  16.3 us
    all_to_all x1, blocking collectives, summed(): return lax.all_to_all(spread, 'gx', 0, 0).reshape(values.shape)  11.3 us
    ppermute x1, starting transfers between devices, shards(): from_below = lax.ppermute(y_high, 'gy', up_y)  4.91 us
    ppermute x1, starting transfers between devices, shards(): other = lax.ppermute(mine, 'gy', swap)  4.2 us
    ppermute x1, waiting for transfers between devices, shards(): from_right = lax.ppermute(x_low, 'gx', [(b, a) for a, b in up_x])  3.59 us
  transfers between devices with their start and end apart: 6, of which 4 were waited for; matrix products, arithmetic and copies ran while one was open for 0% of the time, Pallas kernels for 0%

profile of v1, /device:TPU:1, one launch (start us, length us, event | category | flops | bytes accessed | tf_op | source)
XLA Modules:
  0.0 113.0 jit_solution(8838683568738709089)
XLA Ops:
  0.6 2.0 %faces.1 = (f32[128,128]{1,0:T(8,128)}, f32[128,128]{1,0:T(8,128)}, f32[144,128]{1,0:T(8,128)}, f32[144,128]{1,0:T(8,128)}) custom-call(f32[2048,128]{1,0:T(8,128)} %bitcast.9, f32[256,32]{1,0:T(8,128)} %bitcast.15), custom_call_target="tpu_custom_call" | custom-call | tf_op jit(solution)/shard_map/faces/pallas_call | solution.py:242
  2.7 4.9 %collective-permute-start.2 = (f32[144,128]{1,0:T(8,128)}, f32[144,128]{1,0:T(8,128)S(1)}, u32[]{:S(2)}, u32[]{:S(2)}) collective-permute-start(f32[144,128]{1,0:T(8,128)} %get-tuple-element.17), channel_id=1, source_target_pairs={{0,1},{1,2},{2,3},{3,4},{4,5},{5,6},{6,7},{7,8},{8,9},{9,10},{10,1... | collective-permute-start | bytes 221192 | tf_op jit(solution)/shard_map/ppermute | solution.py:253
  7.6 1.9 %collective-permute-start.3 = (f32[144,128]{1,0:T(8,128)}, f32[144,128]{1,0:T(8,128)S(1)}, u32[]{:S(2)}, u32[]{:S(2)}) collective-permute-start(f32[144,128]{1,0:T(8,128)} %get-tuple-element.18), channel_id=1, source_target_pairs={{1,0},{2,1},{3,2},{4,3},{5,4},{6,5},{7,6},{8,7},{9,8},{10,9},{11,1... | collective-permute-start | bytes 221192 | tf_op jit(solution)/shard_map/ppermute | solution.py:254
  9.5 3.2 %collective-permute-start = (f32[128,128]{1,0:T(8,128)}, f32[128,128]{1,0:T(8,128)S(1)}, u32[]{:S(2)}, u32[]{:S(2)}) collective-permute-start(f32[128,128]{1,0:T(8,128)} %get-tuple-element.15), channel_id=1, source_target_pairs={{0,16},{16,32},{32,48},{48,64},{64,80},{80,96},{96,112},{112,128},... | collective-permute-start | bytes 196616 | tf_op jit(solution)/shard_map/ppermute | solution.py:251
  12.7 1.3 %collective-permute-start.1 = (f32[128,128]{1,0:T(8,128)}, f32[128,128]{1,0:T(8,128)S(1)}, u32[]{:S(2)}, u32[]{:S(2)}) collective-permute-start(f32[128,128]{1,0:T(8,128)} %get-tuple-element.16), channel_id=1, source_target_pairs={{16,0},{32,16},{48,32},{64,48},{80,64},{96,80},{112,96},{128,112},... | collective-permute-start | bytes 196616 | tf_op jit(solution)/shard_map/ppermute | solution.py:252
  14.0 0.3 collective-permute-done.from_left
  14.4 3.6 %collective-permute-done.1.from_right = f32[128,128]{1,0:T(8,128)S(1)} collective-permute-done((f32[128,128]{1,0:T(8,128)}, f32[128,128]{1,0:T(8,128)S(1)}, u32[]{:S(2)}, u32[]{:S(2)}) %collective-permute-start.1) | collective-permute-done | bytes 65568 | tf_op jit(solution)/shard_map/ppermute | solution.py:252
  18.0 0.0 collective-permute-done.2.from_below
  18.0 0.0 collective-permute-done.3.from_above
  18.0 0.0 copy-start.3
  18.0 0.6 copy-done.5
  18.6 0.0 copy-done.2
  18.6 0.0 copy-done.3
  18.6 16.3 %images.1 = (f32[768,128]{1,0:T(8,128)}, f32[768,128]{1,0:T(8,128)}, f32[2048,128]{1,0:T(8,128)}) custom-call(s32[1]{0:T(128)} %bitcast.me.refs_0_, f32[4]{0:T(128)} %weights.1, f32[2048,128]{1,0:T(8,128)} %bitcast.10, f32[256,32]{1,0:T(8,128)} %bitcast.16, f32[128,128]{1,0:T(8,128)} %copy-done.4, f32[128,128]{1,0:T(8,128)} %copy-done.5, ...), custom_call_target="tpu_custom_call" | custom-call | tf_op jit(solution)/shard_map/images/pallas_call | solution.py:257
  34.9 0.0 collective-permute-start.4
  34.9 1.9 %collective-permute-done.4 = f32[768,128]{1,0:T(8,128)S(1)} collective-permute-done((f32[768,128]{1,0:T(8,128)}, f32[768,128]{1,0:T(8,128)S(1)}, u32[]{:S(2)}, u32[]{:S(2)}) %collective-permute-start.4) | collective-permute-done | bytes 393248 | tf_op jit(solution)/shard_map/ppermute | solution.py:275
  36.8 1.1 add.8
  37.9 17.0 %all_to_all.15 = f32[16,48,128]{2,1,0:T(8,128)S(1)} all-to-all(f32[16,48,128]{2,1,0:T(8,128)S(1)} %bitcast.14), channel_id=1, replica_groups=mesh['gx'=16,'gy'=16] {'gx'}, dimensions={0} | all-to-all | bytes 786432 | tf_op jit(solution)/shard_map/all_to_all | solution.py:221
  55.0 19.2 %all_to_all.16 = f32[8,48,128]{2,1,0:T(8,128)S(1)} all-to-all(f32[8,48,128]{2,1,0:T(8,128)S(1)} %broadcast_in_dim.4), channel_id=1, replica_groups={{0,2,4,6,8,10,12,14},{1,3,5,7,9,11,13,15},{16,18,20,22,24,26,28,30},{17..., dimensions={0} | all-to-all | bytes 393216 | tf_op jit(solution)/shard_map/all_to_all | solution.py:224
  74.2 11.3 %all_to_all.17 = f32[16,48,128]{2,1,0:T(8,128)S(1)} all-to-all(f32[16,48,128]{2,1,0:T(8,128)S(1)} %broadcast_in_dim.5), channel_id=1, replica_groups=mesh['gx'=16,'gy'=16] {'gx'}, dimensions={0} | all-to-all | bytes 786432 | tf_op jit(solution)/shard_map/all_to_all | solution.py:226
  85.5 4.2 %collective-permute-start.5 = (f32[768,128]{1,0:T(8,128)S(1)}, f32[768,128]{1,0:T(8,128)S(1)}, u32[]{:S(2)}, u32[]{:S(2)}) collective-permute-start(f32[768,128]{1,0:T(8,128)S(1)} %bitcast.12), channel_id=1, source_target_pairs={{0,1},{1,0},{2,3},{3,2},{4,5},{5,4},{6,7},{7,6},{8,9},{9,8},{10,11... | collective-permute-start | bytes 1179656 | tf_op jit(solution)/shard_map/ppermute | solution.py:277
  89.7 1.3 %collective-permute-done.5.refs_2_ = f32[768,128]{1,0:T(8,128)S(1)} collective-permute-done((f32[768,128]{1,0:T(8,128)S(1)}, f32[768,128]{1,0:T(8,128)S(1)}, u32[]{:S(2)}, u32[]{:S(2)}) %collective-permute-start.5) | collective-permute-done | bytes 393248 | tf_op jit(solution)/shard_map/ppermute | solution.py:277
  91.1 0.7 copy-done.1
  91.8 21.2 %finish.1 = (f32[2048,128]{1,0:T(8,128)}, f32[2048,128]{1,0:T(8,128)}, f32[4,128,128]{2,1,0:T(8,128)}, f32[10,128,128]{2,1,0:T(8,128)}) custom-call(s32[1]{0:T(128)} %bitcast.me.refs_0_, f32[768,128]{1,0:T(8,128)} %bitcast.13, f32[768,128]{1,0:T(8,128)} %copy-done.1, f32[2048,128]{1,0:T(8,128)} %bitcast.11, f32[2048,128]{1,0:T(8,128)} %get-tuple-element.21.refs_4_), custom_call_target="tpu_custom_call" | custom-call | tf_op jit(solution)/shard_map/finish/pallas_call | solution.py:282
  (11 shorter events, 0.1 us)
Async XLA Ops:
  2.7 15.3 %collective-permute-start.2 = (f32[144,128]{1,0:T(8,128)}, f32[144,128]{1,0:T(8,128)S(1)}, u32[]{:S(2)}, u32[]{:S(2)}) collective-permute-start(f32[144,128]{1,0:T(8,128)} %get-tuple-element.17), channel_id=1, source_target_pairs={{0,1},{1,2},{2,3},{3,4},{4,5},{5,6},{6,7},{7,8},{8,9},{9,10},{10,1... | collective-permute-start | bytes 221192 | tf_op jit(solution)/shard_map/ppermute | solution.py:253
  7.6 10.4 %collective-permute-start.3 = (f32[144,128]{1,0:T(8,128)}, f32[144,128]{1,0:T(8,128)S(1)}, u32[]{:S(2)}, u32[]{:S(2)}) collective-permute-start(f32[144,128]{1,0:T(8,128)} %get-tuple-element.18), channel_id=1, source_target_pairs={{1,0},{2,1},{3,2},{4,3},{5,4},{6,5},{7,6},{8,7},{9,8},{10,9},{11,1... | collective-permute-start | bytes 221192 | tf_op jit(solution)/shard_map/ppermute | solution.py:254
  9.5 4.8 %collective-permute-start = (f32[128,128]{1,0:T(8,128)}, f32[128,128]{1,0:T(8,128)S(1)}, u32[]{:S(2)}, u32[]{:S(2)}) collective-permute-start(f32[128,128]{1,0:T(8,128)} %get-tuple-element.15), channel_id=1, source_target_pairs={{0,16},{16,32},{32,48},{48,64},{64,80},{80,96},{96,112},{112,128},... | collective-permute-start | bytes 196616 | tf_op jit(solution)/shard_map/ppermute | solution.py:251
  12.7 5.2 %collective-permute-start.1 = (f32[128,128]{1,0:T(8,128)}, f32[128,128]{1,0:T(8,128)S(1)}, u32[]{:S(2)}, u32[]{:S(2)}) collective-permute-start(f32[128,128]{1,0:T(8,128)} %get-tuple-element.16), channel_id=1, source_target_pairs={{16,0},{32,16},{48,32},{64,48},{80,64},{96,80},{112,96},{128,112},... | collective-permute-start | bytes 196616 | tf_op jit(solution)/shard_map/ppermute | solution.py:252
  14.4 3.6 %copy-start.4 = (f32[128,128]{1,0:T(8,128)}, f32[128,128]{1,0:T(8,128)S(1)}, u32[]{:S(2)}) copy-start(f32[128,128]{1,0:T(8,128)S(1)} %collective-permute-done.from_left) | copy-start | bytes 196612
  17.9 0.6 copy-start.5
  18.0 0.6 copy-start.2
  18.0 0.7 copy-start.3
  34.9 1.9 %collective-permute-start.4 = (f32[768,128]{1,0:T(8,128)}, f32[768,128]{1,0:T(8,128)S(1)}, u32[]{:S(2)}, u32[]{:S(2)}) collective-permute-start(f32[768,128]{1,0:T(8,128)} %get-tuple-element.20), channel_id=1, source_target_pairs={{0,1},{1,0},{2,3},{3,2},{4,5},{5,4},{6,7},{7,6},{8,9},{9,8},{10,11... | collective-permute-start | bytes 1179656 | tf_op jit(solution)/shard_map/ppermute | solution.py:275
  85.5 5.6 %copy-start = (f32[16,48,128]{2,1,0:T(8,128)}, f32[16,48,128]{2,1,0:T(8,128)S(1)}, u32[]{:S(2)}) copy-start(f32[16,48,128]{2,1,0:T(8,128)S(1)} %all_to_all.17) | copy-start | bytes 1179652
  85.5 5.6 %collective-permute-start.5 = (f32[768,128]{1,0:T(8,128)S(1)}, f32[768,128]{1,0:T(8,128)S(1)}, u32[]{:S(2)}, u32[]{:S(2)}) collective-permute-start(f32[768,128]{1,0:T(8,128)S(1)} %bitcast.12), channel_id=1, source_target_pairs={{0,1},{1,0},{2,3},{3,2},{4,5},{5,4},{6,7},{7,6},{8,9},{9,8},{10,11... | collective-permute-start | bytes 1179656 | tf_op jit(solution)/shard_map/ppermute | solution.py:277
  91.1 0.7 copy-start.1

commit v2 on v1

v2 whole, which is shorter than its diff:
```python
import jax
import jax.numpy as jnp
from jax import lax
from jax.experimental import pallas as pl
from jax.experimental.pallas import tpu as pltpu
from jax.sharding import PartitionSpec as P

R = 128
TERMS = 4
operator_pairs = ((0, 0), (0, 1), (0, 2), (0, 3), (1, 1), (1, 2), (1, 3), (2, 2), (2, 3), (3, 3))
crossed_pairs = tuple(pair for pair in operator_pairs if pair[0] != pair[1])
HIGHEST = lax.Precision.HIGHEST
f32, bf16 = jnp.float32, jnp.bfloat16

HALF_SLOTS = 6
HALF = HALF_SLOTS * R
SLAB = 64
WIDTH = (TERMS + 1) * R
BLOCK = 32
halves = (
    ([(0, k + 1) for k in range(TERMS)], [(a + 1, b + 1) for a, b in crossed_pairs[:3]]),
    ([(k + 1, k + 1) for k in range(TERMS)], [(a + 1, b + 1) for a, b in crossed_pairs[3:]]),
)

def faces_kernel(basis, coef, x_low, x_high, y_low, y_high):
    lane = lax.broadcasted_iota(jnp.int32, (SLAB, R), 1)
    slabs = basis.shape[0] // SLAB
    x_low[0:SLAB, :] = basis[0:SLAB, :]
    x_high[0:SLAB, :] = basis[(slabs - 1) * SLAB : slabs * SLAB, :]
    low = jnp.zeros((SLAB, R), f32)
    high = jnp.zeros((SLAB, R), f32)
    for k in range(TERMS):
        rows = coef[k * SLAB : (k + 1) * SLAB, :]
        low = jnp.where(lane == k, rows[:, 0:1], low)
        high = jnp.where(lane == k, rows[:, slabs - 1 : slabs], high)
    x_low[SLAB : 2 * SLAB, :] = low
    x_high[SLAB : 2 * SLAB, :] = high
    for x in range(slabs):
        y_low[4 * x : 4 * x + 4, :] = basis[x * SLAB : x * SLAB + 4, :]
        y_high[4 * x : 4 * x + 4, :] = basis[x * SLAB + SLAB - 4 : (x + 1) * SLAB, :]
    y_low[4 * slabs :, :] = jnp.zeros((16, R), f32)
    y_high[4 * slabs :, :] = jnp.zeros((16, R), f32)
    for k in range(TERMS):
        y_low[4 * (slabs + k) : 4 * (slabs + k) + 4, 0:slabs] = coef[k * SLAB : k * SLAB + 4, :]
        y_high[4 * (slabs + k) : 4 * (slabs + k) + 4, 0:slabs] = coef[(k + 1) * SLAB - 4 : (k + 1) * SLAB, :]


def images_kernel(
    me, nominal_weights, basis, coef, from_left, from_right, from_below, from_above, mine, other, nominal,
    turned, above, below, face, top, bottom, product, squares, total,
):
    slabs = basis.shape[0] // SLAB
    groups = slabs // 2

    def slab(x):
        return basis[x * SLAB : (x + 1) * SLAB, :]

    for j in range(groups):
        turned[j + 1] = jnp.concatenate([slab(j), slab(j + groups)], axis=0).T
    turned[0] = jnp.concatenate([from_left[0:SLAB, :], slab(groups - 1)], axis=0).T
    turned[groups + 1] = jnp.concatenate([slab(groups), from_right[0:SLAB, :]], axis=0).T
    above[...] = from_above[0 : 4 * slabs, :].T
    below[...] = from_below[0 : 4 * slabs, :].T

    spot = lax.broadcasted_iota(jnp.int32, (groups, R), 1) % SLAB
    first = lax.broadcasted_iota(jnp.int32, (groups, R), 1) < SLAB
    group = lax.broadcasted_iota(jnp.int32, (groups, R), 0)
    level = spot % 4

    def joined(rows):
        return jnp.where(first, rows[0:groups], pltpu.roll(rows[groups:slabs], SLAB, 1))

    def flipped(tile):
        return jnp.concatenate([tile, jnp.zeros((R - tile.shape[0], R), f32)], axis=0).T

    left_coef = flipped(from_left[SLAB : 2 * SLAB, :])
    right_coef = flipped(from_right[SLAB : 2 * SLAB, :])
    above_coef = flipped(from_above[4 * slabs :, :])
    below_coef = flipped(from_below[4 * slabs :, :])
    for k in range(TERMS):
        rows = jnp.concatenate([coef[k * SLAB : (k + 1) * SLAB, :], jnp.zeros((SLAB, R - slabs), f32)], axis=1)
        own = joined(flipped(rows))
        half = pltpu.roll(own, SLAB, 1)
        left = jnp.where(first, left_coef[k : k + 1, :], half[groups - 1 : groups, :])
        left = jnp.where(group == 0, left, pltpu.roll(own, 1, 0))
        right = jnp.where(first, half[0:1, :], pltpu.roll(right_coef[k : k + 1, :], SLAB, 1))
        right = jnp.where(group == groups - 1, right, pltpu.roll(own, groups - 1, 0))
        up = jnp.where(
            spot < SLAB - 4,
            pltpu.roll(own, R - 4, 1),
            joined(pltpu.roll(above_coef, SLAB - 4 - 4 * k, 1)),
        )
        down = jnp.where(spot < 4, joined(pltpu.roll(below_coef, (R - 4 * k) % R, 1)), pltpu.roll(own, 4, 1))
        face[0, k] = 0.5 * (own + left)
        face[1, k] = 0.5 * (own + right)
        face[2, k] = 0.5 * (own + up)
        face[3, k] = 0.5 * (own + down)
        face[4, k] = 0.5 * (own + jnp.where(level < 3, pltpu.roll(own, R - 1, 1), 0.0))
        face[5, k] = 0.5 * (own + jnp.where(level > 0, pltpu.roll(own, 1, 1), 0.0))

    squares[...] = jnp.zeros_like(squares)
    lane = lax.broadcasted_iota(jnp.int32, (BLOCK, R), 1)
    inside = lane % SLAB
    depth = lane % 4

    def images(chunk, slot):
        for s in range(2):
            j = 2 * chunk + s
            weights = [[face[f, k, j : j + 1, :] for f in range(6)] for k in range(TERMS)]
            for start in range(0, R, BLOCK):
                rows = slice(start, start + BLOCK)
                v = turned[j + 1, rows, :]
                up = pltpu.roll(above[rows, :], (SLAB - 4 - 4 * j) % R, 1)
                down = pltpu.roll(below[rows, :], (R - 4 * j) % R, 1)
                steps = (
                    v - turned[j, rows, :],
                    v - turned[j + 2, rows, :],
                    v - jnp.where(inside < SLAB - 4, pltpu.roll(v, R - 4, 1), up),
                    v - jnp.where(inside < 4, down, pltpu.roll(v, 4, 1)),
                    v - jnp.where(depth < 3, pltpu.roll(v, R - 1, 1), 0.0),
                    v - jnp.where(depth > 0, pltpu.roll(v, 1, 1), 0.0),
                )
                summed_images = None
                for block in range(TERMS + 1):
                    if block == 0:
                        value = v
                    else:
                        k = block - 1
                        value = weights[k][0] * steps[0]
                        for weight, step in zip(weights[k][1:], steps[1:]):
                            value = value + weight * step
                        part = nominal_weights[k] * value
                        summed_images = part if summed_images is None else summed_images + part
                    high = value.astype(bf16)
                    rest = value - high.astype(f32)
                    squares[block, rows, :] += rest * rest
                    out = slice(block * R + start, block * R + start + BLOCK)
                    top[slot, out, s * R : (s + 1) * R] = high
                    bottom[slot, out, s * R : (s + 1) * R] = rest.astype(bf16)
                total[rows, :] = summed_images
            back = total[...].T
            nominal[j * SLAB : (j + 1) * SLAB, :] = back[0:SLAB]
            nominal[(j + groups) * SLAB : (j + groups + 1) * SLAB, :] = back[SLAB:]

    def grams(chunk, slot):
        for start in range(0, 2 * WIDTH, 256):
            rows = min(start + 256, WIDTH)
            if start + 256 <= WIDTH:
                right = top[slot, start : start + 256, :]
            elif start < WIDTH:
                right = jnp.concatenate([top[slot, start:WIDTH, :], bottom[slot, 0 : start + 256 - WIDTH, :]], axis=0)
            else:
                right = bottom[slot, start - WIDTH : start + 256 - WIDTH, :]
            value = lax.dot_general(
                top[slot, 0:rows, :], right, (((1,), (1,)), ((), ())), preferred_element_type=f32
            )
            if chunk == 0:
                product[0:rows, start : start + 256] = value
            else:
                product[0:rows, start : start + 256] += value

    chunks = groups // 2
    for chunk in range(chunks):
        images(chunk, chunk % 2)
        if chunk > 0:
            grams(chunk - 1, (chunk - 1) % 2)
    grams(chunks - 1, (chunks - 1) % 2)

    r = lax.broadcasted_iota(jnp.int32, (R, R), 0)
    c = lax.broadcasted_iota(jnp.int32, (R, R), 1)

    def gram(a, b):
        high = product[a * R : (a + 1) * R, b * R : (b + 1) * R]
        one = product[a * R : (a + 1) * R, WIDTH + b * R : WIDTH + (b + 1) * R]
        two = product[b * R : (b + 1) * R, WIDTH + a * R : WIDTH + (a + 1) * R]
        if a != b:
            return high + one, two
        return high + one + jnp.where(r == c, jnp.sum(squares[a], axis=1, keepdims=True), 0.0), two

    def symmetric(a, b):
        one, two = gram(a, b)
        return one + two.T

    def diagonal(matrix):
        return jnp.sum(jnp.where(c == r, matrix, 0.0), axis=0, keepdims=True)

    base = symmetric(0, 0)
    for h, (even, full) in enumerate(halves):
        zero, one, two, three = [symmetric(*pair) for pair in even]
        tiles = [jnp.where(c >= r, base, zero), jnp.where(c >= r, one, two), jnp.where(c >= r, three, 0.0)]
        lines = []
        for line in (diagonal(zero), diagonal(two)):
            lines += [line, pltpu.roll(line, SLAB, 1)]
        for q, line in enumerate(lines):
            tiles[2] = jnp.where((r == R - 1 - q) & (c < SLAB), line, tiles[2])
        for pair in full:
            high, low = gram(*pair)
            tiles.append(high.T + low)

        def store(target, tiles=tiles):
            for q, tile in enumerate(tiles):
                target[q * R : (q + 1) * R, :] = tile

        pl.when(me[0] == h)(lambda: store(mine))
        pl.when(me[0] != h)(lambda: store(other))


def spread(value):
    return jnp.broadcast_to(value, (8, R))


def stacked(values, row8):
    out = values[-1]
    for i in range(len(values) - 2, -1, -1):
        out = jnp.where(row8 == i, values[i], out)
    return out


def panel_factor(rows, start):
    column = [spread(rows[:, start + l : start + l + 1]) for l in range(8)]
    a = [[spread(column[l][i : i + 1, :]) for l in range(i + 1)] for i in range(8)]
    inverse_pivot = [None] * 8
    lower = [[None] * 8 for _ in range(8)]
    for j in range(8):
        inverse_pivot[j] = 1.0 / a[j][j]
        for i in range(j + 1, 8):
            lower[i][j] = a[i][j] * inverse_pivot[j]
        for i in range(j + 1, 8):
            for l in range(j + 1, i + 1):
                a[i][l] = a[i][l] - lower[i][j] * a[l][j]
    turn = [[None] * 8 for _ in range(8)]
    for j in range(8):
        for i in range(j + 1, 8):
            value = lower[i][j]
            for l in range(j + 1, i):
                value = value + lower[i][l] * turn[l][j]
            turn[i][j] = -value
    return [a[j][j] for j in range(8)], inverse_pivot, turn


def factor_kernel(slot, inverse_t, inverse, *, cells):
    r = lax.broadcasted_iota(jnp.int32, (R, R), 0)
    c = lax.broadcasted_iota(jnp.int32, (R, R), 1)
    gram = jnp.where(c >= r, slot[...], slot[...].T) * (1.0 / cells)
    row8 = lax.broadcasted_iota(jnp.int32, (8, R), 0)
    lane8 = lax.broadcasted_iota(jnp.int32, (8, R), 1)
    panels = R // 8
    left = [gram[8 * i : 8 * i + 8, :] for i in range(panels)]
    right = [jnp.where(row8 + 8 * i == lane8, 1.0, 0.0).astype(f32) for i in range(panels)]
    for p in range(panels):
        start = 8 * p
        pivots, inverse_pivots, turn = panel_factor(left[p], start)
        ends = []
        for rows in (left[p], right[p]):
            out = rows
            for l in range(7):
                weight = jnp.where(row8 > l, turn[7][l], 0.0)
                for i in range(l + 1, 7):
                    weight = jnp.where(row8 == i, turn[i][l], weight)
                out = out + weight * spread(rows[l : l + 1, :])
            ends.append(out)
        inverse[start : start + 8, :] = ends[1] * stacked([1.0 / jnp.sqrt(pivot) for pivot in pivots], row8)
        if p == panels - 1:
            break
        scale = stacked(inverse_pivots, row8)
        solved = []
        for rows in ends:
            rows = rows * scale
            out = rows
            for i in range(1, 8):
                weight = jnp.where(row8 == 0, turn[i][0], 0.0)
                for l in range(1, i):
                    weight = jnp.where(row8 == l, turn[i][l], weight)
                out = out + weight * spread(rows[i : i + 1, :])
            solved.append(out)
        weights = [spread(left[p + 1][:, start + l : start + l + 1]) for l in range(8)]
        rest = left[p + 2 :]
        updates = []
        for out in solved:
            terms = [weights[l] * spread(out[l : l + 1, :]) for l in range(8)]
            while len(terms) > 1:
                terms = [terms[i] + terms[i + 1] for i in range(0, len(terms), 2)]
            updates.append(terms[0])
        left[p + 1] = left[p + 1] - updates[0]
        right[p + 1] = right[p + 1] - updates[1]
        if rest:
            columns = jnp.concatenate(rest, axis=0)[:, start : start + 8]
            update = jnp.dot(columns, jnp.concatenate(solved, axis=1), precision=HIGHEST, preferred_element_type=f32)
            for i in range(p + 2, panels):
                q = 8 * (i - p - 2)
                left[i] = left[i] - update[q : q + 8, :R]
                right[i] = right[i] - update[q : q + 8, R:]
    inverse_t[...] = inverse[...].T


def parts(value, count):
    out = []
    for _ in range(count):
        out.append(value.astype(bf16))
        value = value - out[-1].astype(f32)
    return out


def finish_kernel(
    me, mine, other, basis, nominal, inverse_t, ortho_out, nominal_out, reduced_out, residual_out, packed, *, cells
):
    packed[pl.ds(pl.multiple_of(me[0] * HALF, R), HALF), :] = mine[...]
    packed[pl.ds(pl.multiple_of((1 - me[0]) * HALF, R), HALF), :] = other[...]
    high, middle, low = parts(inverse_t[...], 3)
    line = jnp.concatenate([high, middle], axis=1)
    square = jnp.concatenate([line, line], axis=0)
    last = jnp.concatenate([high, low], axis=0)

    def short(value):
        one, two = parts(value, 2)
        out = jnp.dot(jnp.concatenate([one, two], axis=1), square, preferred_element_type=f32)
        return out[:, :R] + out[:, R:]

    def product(value):
        one, two, three = parts(value, 3)
        out = jnp.dot(jnp.concatenate([one, two], axis=1), square, preferred_element_type=f32)
        end = jnp.dot(jnp.concatenate([three, one], axis=1), last, preferred_element_type=f32)
        return out[:, :R] + (out[:, R:] + end)

    step = 512
    for source, target in ((basis, ortho_out), (nominal, nominal_out)):
        for start in range(0, basis.shape[0], step):
            target[start : start + step, :] = short(source[start : start + step, :])

    r = lax.broadcasted_iota(jnp.int32, (R, R), 0)
    c = lax.broadcasted_iota(jnp.int32, (R, R), 1)
    scale = 1.0 / cells

    def moved(matrix):
        return product(product(matrix * scale).T)

    for h, (even, full) in enumerate(halves):
        tiles = [packed[h * HALF + q * R : h * HALF + (q + 1) * R, :] for q in range(HALF_SLOTS)]
        turned = [tile.T for tile in tiles[:3]]
        lines = []
        for q in range(2):
            one = tiles[2][R - 1 - 2 * q : R - 2 * q, :]
            two = pltpu.roll(tiles[2][R - 2 - 2 * q : R - 1 - 2 * q, :], SLAB, 1)
            lines.append(jnp.where(c[0:1] < SLAB, one, two))
        matrices = [
            jnp.where(c < r, tiles[0], jnp.where(c == r, lines[0], turned[0])),
            jnp.where(c >= r, tiles[1], turned[1]),
            jnp.where(c < r, tiles[1], jnp.where(c == r, lines[1], turned[1])),
            jnp.where(c >= r, tiles[2], turned[2]),
        ] + tiles[3:]
        for (a, b), matrix in zip(even + full, matrices):
            if a == 0:
                reduced_out[b - 1] = moved(matrix)
            else:
                residual_out[operator_pairs.index((a - 1, b - 1))] = moved(matrix)


def summed(values, groups):
    count = lax.axis_size("gx")
    width = values.shape[1]
    parts = values.reshape(count, -1, width)
    shard = jnp.sum(lax.all_to_all(parts, "gx", 0, 0), axis=0)
    depth = len(groups[0])
    along = jnp.broadcast_to(shard[None], (depth,) + shard.shape)
    shard = jnp.sum(lax.all_to_all(along, "gy", 0, 0, axis_index_groups=groups), axis=0)
    spread = jnp.broadcast_to(shard[None], (count,) + shard.shape)
    return lax.all_to_all(spread, "gx", 0, 0).reshape(values.shape)


def shards(raw_basis, coefficients, nominal_weights):
    nx, ny, nz, width = raw_basis.shape
    count_x, count_y = lax.axis_size("gx"), lax.axis_size("gy")
    cells = nx * ny * nz * count_x * count_y
    flat = raw_basis.reshape(-1, width)
    coef = jnp.transpose(coefficients, (0, 2, 3, 1)).reshape(-1, nx)
    vmem = pl.BlockSpec(memory_space=pltpu.VMEM)
    smem = pl.BlockSpec(memory_space=pltpu.SMEM)

    def array(*shape):
        return jax.ShapeDtypeStruct(shape, f32)

    y_rows = 4 * nx + 4 * TERMS
    x_low, x_high, y_low, y_high = pl.pallas_call(
        faces_kernel,
        out_shape=(array(2 * SLAB, R), array(2 * SLAB, R), array(y_rows, R), array(y_rows, R)),
        in_specs=[vmem, vmem],
        out_specs=(vmem,) * 4,
        name="faces",
    )(flat, coef)
    up_x = [(i, i + 1) for i in range(count_x - 1)]
    up_y = [(i, i + 1) for i in range(count_y - 1)]
    from_left = lax.ppermute(x_high, "gx", up_x)
    from_right = lax.ppermute(x_low, "gx", [(b, a) for a, b in up_x])
    from_below = lax.ppermute(y_high, "gy", up_y)
    from_above = lax.ppermute(y_low, "gy", [(b, a) for a, b in up_y])

    me = (lax.axis_index("gy") % 2).astype(jnp.int32).reshape(1)
    groups = nx // 2
    mine, other, raw_nominal = pl.pallas_call(
        images_kernel,
        out_shape=(array(HALF, R), array(HALF, R), array(nx * SLAB, R)),
        in_specs=[smem, smem] + [vmem] * 6,
        out_specs=(vmem,) * 3,
        scratch_shapes=[
            pltpu.VMEM((groups + 2, R, R), f32),
            pltpu.VMEM((R, 4 * nx), f32),
            pltpu.VMEM((R, 4 * nx), f32),
            pltpu.VMEM((6, TERMS, groups, R), f32),
            pltpu.VMEM((2, WIDTH, 2 * R), bf16),
            pltpu.VMEM((2, WIDTH, 2 * R), bf16),
            pltpu.VMEM((WIDTH, 2 * WIDTH), f32),
            pltpu.VMEM((TERMS + 1, R, R), f32),
            pltpu.VMEM((R, R), f32),
        ],
        name="images",
    )(me, nominal_weights, flat, coef, from_left, from_right, from_below, from_above)

    swap = [(i, i ^ 1) for i in range(count_y)]
    along_z = [list(range(core, count_y, 2)) for core in range(2)]
    mine = mine + lax.ppermute(other, "gy", swap)
    mine = summed(mine, along_z)
    other = lax.ppermute(mine, "gy", swap)

    def factor(*refs):
        factor_kernel(*refs, cells=cells)

    def finish(*refs):
        finish_kernel(*refs, cells=cells)

    inverse_t = pl.pallas_call(
        factor,
        out_shape=array(R, R),
        grid=(1,),
        in_specs=[pl.BlockSpec((R, R), lambda i: (0, 0))],
        out_specs=pl.BlockSpec((R, R), lambda i: (0, 0)),
        scratch_shapes=[pltpu.VMEM((R, R), f32)],
        name="factor",
    )(mine)
    ortho, nominal, reduced_ops, residual_grams = pl.pallas_call(
        finish,
        out_shape=(array(nx * SLAB, R), array(nx * SLAB, R), array(TERMS, R, R), array(len(operator_pairs), R, R)),
        in_specs=[smem] + [vmem] * 5,
        out_specs=(vmem,) * 4,
        scratch_shapes=[pltpu.VMEM((2 * HALF, R), f32)],
        name="finish",
    )(me, mine, other, flat, raw_nominal, inverse_t)
    shape = raw_basis.shape
    return (ortho.reshape(shape), nominal.reshape(shape), reduced_ops, residual_grams)


def solution(mesh):
    in_specs = (P("gx", "gy", None, None), P(None, "gx", "gy", None), P())
    out_specs = (P("gx", "gy", None, None), P("gx", "gy", None, None), P(), P())
    return jax.shard_map(shards, mesh=mesh, in_specs=in_specs, out_specs=out_specs, check_vma=False)
```

time: 113 us -> 96.6 us (0.85)
  Pallas kernels: 39.5 us -> 24 us
  waiting for transfers between devices: 7.19 us -> 5.85 us
    pallas_call x1, Pallas kernels: 21.2 us -> 6.91 us  [shards(): pl.pallas_call(finish, out_shape=(array(nx * SLAB, R), array(nx * SLAB, R...]
    pallas_call x1, Pallas kernels: 16.3 us -> 8.99 us  [shards(): pl.pallas_call(images_kernel, out_shape=(array(HALF, R), array(HALF, R),...]
    pallas_call x0 -> x1, Pallas kernels: none -> 6.08 us  [shards(): pl.pallas_call(factor, out_shape=array(R, R), grid=(1,), in_specs=[pl.Blo...]
    ppermute x1, waiting for transfers between devices: 1.35 us -> 0.01 us  [shards(): other = lax.ppermute(mine, 'gy', swap)]
  transfers between devices with their start and end apart: 6 -> 6, of which waited for: 4 -> 3; matrix products, arithmetic and copies ran while one was open for 0% -> 0% of each run, Pallas kernels for 0% -> 6%
where the time goes in v2:
time: 96.6 us; the launch traced here: 96.2 us
  blocking collectives  47.5 us (49%)
  Pallas kernels  24 us (25%)
  starting transfers between devices  15.5 us (16%)
  waiting for transfers between devices  5.85 us (6%)
  local copies, waits for them, and re-layouts  1.44 us (1%)
  other arithmetic  1.1 us (1%)
    all_to_all x1, blocking collectives, summed(): lax.all_to_all(along, 'gy', 0, 0, axis_index_groups=groups)  19.2 us
    all_to_all x1, blocking collectives, summed(): shard = jnp.sum(lax.all_to_all(parts, 'gx', 0, 0), axis=0)  17 us
    all_to_all x1, blocking collectives, summed(): return lax.all_to_all(spread, 'gx', 0, 0).reshape(values.shape)  11.3 us
    pallas_call x1, Pallas kernels, shards(): pl.pallas_call(images_kernel, out_shape=(array(HALF, R), array(HALF, R),...  8.99 us
    pallas_call x1, Pallas kernels, shards(): pl.pallas_call(finish, out_shape=(array(nx * SLAB, R), array(nx * SLAB, R...  6.91 us
    pallas_call x1, Pallas kernels, shards(): pl.pallas_call(factor, out_shape=array(R, R), grid=(1,), in_specs=[pl.Blo...  6.08 us
    ppermute x1, starting transfers between devices, shards(): from_below = lax.ppermute(y_high, 'gy', up_y)  4.91 us
    ppermute x1, starting transfers between devices, shards(): other = lax.ppermute(mine, 'gy', swap)  4.2 us
  transfers between devices with their start and end apart: 6, of which 3 were waited for; matrix products, arithmetic and copies ran while one was open for 0% of the time, Pallas kernels for 6%

profile of v2, /device:TPU:1, one launch (start us, length us, event | category | flops | bytes accessed | tf_op | source)
XLA Modules:
  0.0 96.2 jit_solution(15422861890261060461)
XLA Ops:
  0.6 2.0 %faces.1 = (f32[128,128]{1,0:T(8,128)}, f32[128,128]{1,0:T(8,128)}, f32[144,128]{1,0:T(8,128)}, f32[144,128]{1,0:T(8,128)}) custom-call(f32[2048,128]{1,0:T(8,128)} %bitcast.9, f32[256,32]{1,0:T(8,128)} %bitcast.16), custom_call_target="tpu_custom_call" | custom-call | tf_op jit(solution)/shard_map/faces/pallas_call | solution.py:383
  2.7 4.9 %collective-permute-start.2 = (f32[144,128]{1,0:T(8,128)}, f32[144,128]{1,0:T(8,128)S(1)}, u32[]{:S(2)}, u32[]{:S(2)}) collective-permute-start(f32[144,128]{1,0:T(8,128)} %get-tuple-element.17), channel_id=1, source_target_pairs={{0,1},{1,2},{2,3},{3,4},{4,5},{5,6},{6,7},{7,8},{8,9},{9,10},{10,1... | collective-permute-start | bytes 221192 | tf_op jit(solution)/shard_map/ppermute | solution.py:394
  7.6 1.9 %collective-permute-start.3 = (f32[144,128]{1,0:T(8,128)}, f32[144,128]{1,0:T(8,128)S(1)}, u32[]{:S(2)}, u32[]{:S(2)}) collective-permute-start(f32[144,128]{1,0:T(8,128)} %get-tuple-element.18), channel_id=1, source_target_pairs={{1,0},{2,1},{3,2},{4,3},{5,4},{6,5},{7,6},{8,7},{9,8},{10,9},{11,1... | collective-permute-start | bytes 221192 | tf_op jit(solution)/shard_map/ppermute | solution.py:395
  9.5 3.2 %collective-permute-start = (f32[128,128]{1,0:T(8,128)}, f32[128,128]{1,0:T(8,128)S(1)}, u32[]{:S(2)}, u32[]{:S(2)}) collective-permute-start(f32[128,128]{1,0:T(8,128)} %get-tuple-element.15), channel_id=1, source_target_pairs={{0,16},{16,32},{32,48},{48,64},{64,80},{80,96},{96,112},{112,128},... | collective-permute-start | bytes 196616 | tf_op jit(solution)/shard_map/ppermute | solution.py:392
  12.7 1.3 %collective-permute-start.1 = (f32[128,128]{1,0:T(8,128)}, f32[128,128]{1,0:T(8,128)S(1)}, u32[]{:S(2)}, u32[]{:S(2)}) collective-permute-start(f32[128,128]{1,0:T(8,128)} %get-tuple-element.16), channel_id=1, source_target_pairs={{16,0},{32,16},{48,32},{64,48},{80,64},{96,80},{112,96},{128,112},... | collective-permute-start | bytes 196616 | tf_op jit(solution)/shard_map/ppermute | solution.py:393
  14.0 0.3 collective-permute-done.from_left
  14.4 3.6 %collective-permute-done.1.from_right = f32[128,128]{1,0:T(8,128)S(1)} collective-permute-done((f32[128,128]{1,0:T(8,128)}, f32[128,128]{1,0:T(8,128)S(1)}, u32[]{:S(2)}, u32[]{:S(2)}) %collective-permute-start.1) | collective-permute-done | bytes 65568 | tf_op jit(solution)/shard_map/ppermute | solution.py:393
  18.0 0.0 collective-permute-done.2.from_below
  18.0 0.0 collective-permute-done.3.from_above
  18.0 0.0 copy-start.3
  18.0 0.6 copy-done.5
  18.6 0.0 copy-done.2
  18.6 0.0 copy-done.3
  18.6 9.0 %images.1 = (f32[768,128]{1,0:T(8,128)}, f32[768,128]{1,0:T(8,128)}, f32[2048,128]{1,0:T(8,128)}) custom-call(s32[1]{0:T(128)} %bitcast.me.refs_0_, f32[4]{0:T(128)} %nominal_weights.1, f32[2048,128]{1,0:T(8,128)} %bitcast.10, f32[256,32]{1,0:T(8,128)} %bitcast.17, f32[128,128]{1,0:T(8,128)} %copy-done.4, f32[128,128]{1,0:T(8,128)} %copy-done.5, ...), custom_call_target="tpu_custom_call" | custom-call | tf_op jit(solution)/shard_map/images/pallas_call | solution.py:399
  27.6 0.0 collective-permute-start.4
  27.6 1.9 %collective-permute-done.4 = f32[768,128]{1,0:T(8,128)S(1)} collective-permute-done((f32[768,128]{1,0:T(8,128)}, f32[768,128]{1,0:T(8,128)S(1)}, u32[]{:S(2)}, u32[]{:S(2)}) %collective-permute-start.4) | collective-permute-done | bytes 393248 | tf_op jit(solution)/shard_map/ppermute | solution.py:420
  29.6 1.1 %add.8 = f32[768,128]{1,0:T(8,128)S(1)} add(f32[768,128]{1,0:T(8,128)} %get-tuple-element.19, f32[768,128]{1,0:T(8,128)S(1)} %collective-permute-done.4) | non-fusion elementwise | flops 98304 | bytes 1179648 | tf_op jit(solution)/shard_map/add | solution.py:420
  30.6 17.0 %all_to_all.15 = f32[16,48,128]{2,1,0:T(8,128)S(1)} all-to-all(f32[16,48,128]{2,1,0:T(8,128)S(1)} %bitcast.15), channel_id=1, replica_groups=mesh['gx'=16,'gy'=16] {'gx'}, dimensions={0} | all-to-all | bytes 786432 | tf_op jit(solution)/shard_map/all_to_all | solution.py:362
  47.7 19.2 %all_to_all.16 = f32[8,48,128]{2,1,0:T(8,128)S(1)} all-to-all(f32[8,48,128]{2,1,0:T(8,128)S(1)} %broadcast_in_dim.4), channel_id=1, replica_groups={{0,2,4,6,8,10,12,14},{1,3,5,7,9,11,13,15},{16,18,20,22,24,26,28,30},{17..., dimensions={0} | all-to-all | bytes 393216 | tf_op jit(solution)/shard_map/all_to_all | solution.py:365
  66.9 11.3 %all_to_all.17 = f32[16,48,128]{2,1,0:T(8,128)S(1)} all-to-all(f32[16,48,128]{2,1,0:T(8,128)S(1)} %broadcast_in_dim.5), channel_id=1, replica_groups=mesh['gx'=16,'gy'=16] {'gx'}, dimensions={0} | all-to-all | bytes 786432 | tf_op jit(solution)/shard_map/all_to_all | solution.py:367
  78.2 4.2 %collective-permute-start.5 = (f32[768,128]{1,0:T(8,128)S(1)}, f32[768,128]{1,0:T(8,128)S(1)}, u32[]{:S(2)}, u32[]{:S(2)}) collective-permute-start(f32[768,128]{1,0:T(8,128)S(1)} %bitcast.12), channel_id=1, source_target_pairs={{0,1},{1,0},{2,3},{3,2},{4,5},{5,4},{6,7},{7,6},{8,9},{9,8},{10,11... | collective-permute-start | bytes 1179656 | tf_op jit(solution)/shard_map/ppermute | solution.py:422
  82.4 6.1 %factor.1.refs_5_ = f32[128,128]{1,0:T(8,128)} custom-call(f32[768,128]{1,0:T(8,128)} %bitcast.13), custom_call_target="tpu_custom_call" | custom-call | tf_op jit(solution)/shard_map/factor/pallas_call | solution.py:430
  88.5 0.7 copy-done.1
  89.3 6.9 %finish.1 = (f32[2048,128]{1,0:T(8,128)}, f32[2048,128]{1,0:T(8,128)}, f32[4,128,128]{2,1,0:T(8,128)}, f32[10,128,128]{2,1,0:T(8,128)}) custom-call(s32[1]{0:T(128)} %bitcast.me.refs_0_, f32[768,128]{1,0:T(8,128)} %bitcast.14, f32[768,128]{1,0:T(8,128)} %copy-done.1, f32[2048,128]{1,0:T(8,128)} %bitcast.11, f32[2048,128]{1,0:T(8,128)} %get-tuple-element.21.refs_4_, ...), custom_call_target="tpu_custom_call" | custom-call | tf_op jit(solution)/shard_map/finish/pallas_call | solution.py:439
  (12 shorter events, 0.1 us)
Async XLA Ops:
  2.7 15.3 %collective-permute-start.2 = (f32[144,128]{1,0:T(8,128)}, f32[144,128]{1,0:T(8,128)S(1)}, u32[]{:S(2)}, u32[]{:S(2)}) collective-permute-start(f32[144,128]{1,0:T(8,128)} %get-tuple-element.17), channel_id=1, source_target_pairs={{0,1},{1,2},{2,3},{3,4},{4,5},{5,6},{6,7},{7,8},{8,9},{9,10},{10,1... | collective-permute-start | bytes 221192 | tf_op jit(solution)/shard_map/ppermute | solution.py:394
  7.6 10.4 %collective-permute-start.3 = (f32[144,128]{1,0:T(8,128)}, f32[144,128]{1,0:T(8,128)S(1)}, u32[]{:S(2)}, u32[]{:S(2)}) collective-permute-start(f32[144,128]{1,0:T(8,128)} %get-tuple-element.18), channel_id=1, source_target_pairs={{1,0},{2,1},{3,2},{4,3},{5,4},{6,5},{7,6},{8,7},{9,8},{10,9},{11,1... | collective-permute-start | bytes 221192 | tf_op jit(solution)/shard_map/ppermute | solution.py:395
  9.5 4.8 %collective-permute-start = (f32[128,128]{1,0:T(8,128)}, f32[128,128]{1,0:T(8,128)S(1)}, u32[]{:S(2)}, u32[]{:S(2)}) collective-permute-start(f32[128,128]{1,0:T(8,128)} %get-tuple-element.15), channel_id=1, source_target_pairs={{0,16},{16,32},{32,48},{48,64},{64,80},{80,96},{96,112},{112,128},... | collective-permute-start | bytes 196616 | tf_op jit(solution)/shard_map/ppermute | solution.py:392
  12.7 5.2 %collective-permute-start.1 = (f32[128,128]{1,0:T(8,128)}, f32[128,128]{1,0:T(8,128)S(1)}, u32[]{:S(2)}, u32[]{:S(2)}) collective-permute-start(f32[128,128]{1,0:T(8,128)} %get-tuple-element.16), channel_id=1, source_target_pairs={{16,0},{32,16},{48,32},{64,48},{80,64},{96,80},{112,96},{128,112},... | collective-permute-start | bytes 196616 | tf_op jit(solution)/shard_map/ppermute | solution.py:393
  14.4 3.6 %copy-start.4 = (f32[128,128]{1,0:T(8,128)}, f32[128,128]{1,0:T(8,128)S(1)}, u32[]{:S(2)}) copy-start(f32[128,128]{1,0:T(8,128)S(1)} %collective-permute-done.from_left) | copy-start | bytes 196612
  17.9 0.6 copy-start.5
  18.0 0.6 copy-start.2
  18.0 0.7 copy-start.3
  27.6 1.9 %collective-permute-start.4 = (f32[768,128]{1,0:T(8,128)}, f32[768,128]{1,0:T(8,128)S(1)}, u32[]{:S(2)}, u32[]{:S(2)}) collective-permute-start(f32[768,128]{1,0:T(8,128)} %get-tuple-element.20), channel_id=1, source_target_pairs={{0,1},{1,0},{2,3},{3,2},{4,5},{5,4},{6,7},{7,6},{8,9},{9,8},{10,11... | collective-permute-start | bytes 1179656 | tf_op jit(solution)/shard_map/ppermute | solution.py:420
  78.2 4.2 %copy-start = (f32[16,48,128]{2,1,0:T(8,128)}, f32[16,48,128]{2,1,0:T(8,128)S(1)}, u32[]{:S(2)}) copy-start(f32[16,48,128]{2,1,0:T(8,128)S(1)} %all_to_all.17) | copy-start | bytes 1179652
  78.2 10.3 %collective-permute-start.5 = (f32[768,128]{1,0:T(8,128)S(1)}, f32[768,128]{1,0:T(8,128)S(1)}, u32[]{:S(2)}, u32[]{:S(2)}) collective-permute-start(f32[768,128]{1,0:T(8,128)S(1)} %bitcast.12), channel_id=1, source_target_pairs={{0,1},{1,0},{2,3},{3,2},{4,5},{5,4},{6,7},{7,6},{8,9},{9,8},{10,11... | collective-permute-start | bytes 1179656 | tf_op jit(solution)/shard_map/ppermute | solution.py:422
  88.5 0.7 copy-start.1

commit v3 on v2

--- a/solution.py
+++ b/solution.py
@@ -17,48 +17,78 @@
 SLAB = 64
 WIDTH = (TERMS + 1) * R
 BLOCK = 32
+VMEM_LIMIT = 24 * 2**20
 halves = (
     ([(0, k + 1) for k in range(TERMS)], [(a + 1, b + 1) for a, b in crossed_pairs[:3]]),
     ([(k + 1, k + 1) for k in range(TERMS)], [(a + 1, b + 1) for a, b in crossed_pairs[3:]]),
 )
 
-def faces_kernel(basis, coef, x_low, x_high, y_low, y_high):
+def faces_kernel(me, basis, coef, x_first, x_second, y_first, y_second):
     lane = lax.broadcasted_iota(jnp.int32, (SLAB, R), 1)
     slabs = basis.shape[0] // SLAB
-    x_low[0:SLAB, :] = basis[0:SLAB, :]
-    x_high[0:SLAB, :] = basis[(slabs - 1) * SLAB : slabs * SLAB, :]
-    low = jnp.zeros((SLAB, R), f32)
-    high = jnp.zeros((SLAB, R), f32)
-    for k in range(TERMS):
-        rows = coef[k * SLAB : (k + 1) * SLAB, :]
-        low = jnp.where(lane == k, rows[:, 0:1], low)
-        high = jnp.where(lane == k, rows[:, slabs - 1 : slabs], high)
-    x_low[SLAB : 2 * SLAB, :] = low
-    x_high[SLAB : 2 * SLAB, :] = high
-    for x in range(slabs):
-        y_low[4 * x : 4 * x + 4, :] = basis[x * SLAB : x * SLAB + 4, :]
-        y_high[4 * x : 4 * x + 4, :] = basis[x * SLAB + SLAB - 4 : (x + 1) * SLAB, :]
-    y_low[4 * slabs :, :] = jnp.zeros((16, R), f32)
-    y_high[4 * slabs :, :] = jnp.zeros((16, R), f32)
-    for k in range(TERMS):
-        y_low[4 * (slabs + k) : 4 * (slabs + k) + 4, 0:slabs] = coef[k * SLAB : k * SLAB + 4, :]
-        y_high[4 * (slabs + k) : 4 * (slabs + k) + 4, 0:slabs] = coef[(k + 1) * SLAB - 4 : (k + 1) * SLAB, :]
+
+    def x_faces(low, high):
+        low[0:SLAB, :] = basis[0:SLAB, :]
+        high[0:SLAB, :] = basis[(slabs - 1) * SLAB : slabs * SLAB, :]
+        first = jnp.zeros((SLAB, R), f32)
+        last = jnp.zeros((SLAB, R), f32)
+        for k in range(TERMS):
+            rows = coef[k * SLAB : (k + 1) * SLAB, :]
+            first = jnp.where(lane == k, rows[:, 0:1], first)
+            last = jnp.where(lane == k, rows[:, slabs - 1 : slabs], last)
+        low[SLAB : 2 * SLAB, :] = first
+        high[SLAB : 2 * SLAB, :] = last
+
+    def y_faces(low, high):
+        for x in range(slabs):
+            low[4 * x : 4 * x + 4, :] = basis[x * SLAB : x * SLAB + 4, :]
+            high[4 * x : 4 * x + 4, :] = basis[x * SLAB + SLAB - 4 : (x + 1) * SLAB, :]
+        low[4 * slabs :, :] = jnp.zeros((16, R), f32)
+        high[4 * slabs :, :] = jnp.zeros((16, R), f32)
+        for k in range(TERMS):
+            low[4 * (slabs + k) : 4 * (slabs + k) + 4, 0:slabs] = coef[k * SLAB : k * SLAB + 4, :]
+            high[4 * (slabs + k) : 4 * (slabs + k) + 4, 0:slabs] = coef[(k + 1) * SLAB - 4 : (k + 1) * SLAB, :]
+
+    pl.when(me[1] == 0)(lambda: x_faces(x_second, x_first))
+    pl.when(me[1] != 0)(lambda: x_faces(x_first, x_second))
+    pl.when(me[0] == 0)(lambda: y_faces(y_second, y_first))
+    pl.when(me[0] != 0)(lambda: y_faces(y_first, y_second))
+
+
+def turn_kernel(basis, turned):
+    groups = turned.shape[0]
+    for j in range(groups):
+        one = basis[j * SLAB : (j + 1) * SLAB, :]
+        two = basis[(j + groups) * SLAB : (j + groups + 1) * SLAB, :]
+        turned[j] = jnp.concatenate([one, two], axis=0).T
 
 
 def images_kernel(
-    me, nominal_weights, basis, coef, from_left, from_right, from_below, from_above, mine, other, nominal,
-    turned, above, below, face, top, bottom, product, squares, total,
+    me, nominal_weights, turned, before, after, coef, x_first, x_second, y_first, y_second, mine, other, nominal,
+    from_left, from_right, from_below, from_above, ends, above, below, face, top, bottom, product, squares, total,
 ):
-    slabs = basis.shape[0] // SLAB
-    groups = slabs // 2
-
-    def slab(x):
-        return basis[x * SLAB : (x + 1) * SLAB, :]
-
-    for j in range(groups):
-        turned[j + 1] = jnp.concatenate([slab(j), slab(j + groups)], axis=0).T
-    turned[0] = jnp.concatenate([from_left[0:SLAB, :], slab(groups - 1)], axis=0).T
-    turned[groups + 1] = jnp.concatenate([slab(groups), from_right[0:SLAB, :]], axis=0).T
+    groups = turned.shape[0]
+    slabs = 2 * groups
+
+    def copied(*pairs):
+        for source, target in pairs:
+            target[...] = source[...]
+
+    pl.when(me[1] == 0)(lambda: copied((x_second, from_left), (x_first, from_right)))
+    pl.when(me[1] != 0)(lambda: copied((x_first, from_left), (x_second, from_right)))
+    pl.when(me[0] == 0)(lambda: copied((y_second, from_below), (y_first, from_above)))
+    pl.when(me[0] != 0)(lambda: copied((y_first, from_below), (y_second, from_above)))
+
+    ends[0] = jnp.concatenate([from_left[0:SLAB, :], before[...]], axis=0).T
+    ends[1] = jnp.concatenate([after[...], from_right[0:SLAB, :]], axis=0).T
+
+    def strip(j, rows):
+        if j < 0:
+            return ends[0, rows, :]
+        if j == groups:
+            return ends[1, rows, :]
+        return turned[j, rows, :]
+
     above[...] = from_above[0 : 4 * slabs, :].T
     below[...] = from_below[0 : 4 * slabs, :].T
 
@@ -109,12 +139,12 @@
             weights = [[face[f, k, j : j + 1, :] for f in range(6)] for k in range(TERMS)]
             for start in range(0, R, BLOCK):
                 rows = slice(start, start + BLOCK)
-                v = turned[j + 1, rows, :]
+                v = turned[j, rows, :]
                 up = pltpu.roll(above[rows, :], (SLAB - 4 - 4 * j) % R, 1)
                 down = pltpu.roll(below[rows, :], (R - 4 * j) % R, 1)
                 steps = (
-                    v - turned[j, rows, :],
-                    v - turned[j + 2, rows, :],
+                    v - strip(j - 1, rows),
+                    v - strip(j + 1, rows),
                     v - jnp.where(inside < SLAB - 4, pltpu.roll(v, R - 4, 1), up),
                     v - jnp.where(inside < 4, down, pltpu.roll(v, 4, 1)),
                     v - jnp.where(depth < 3, pltpu.roll(v, R - 1, 1), 0.0),
@@ -379,30 +409,50 @@
     def array(*shape):
         return jax.ShapeDtypeStruct(shape, f32)
 
+    me = jnp.stack([lax.axis_index("gy") % 2, lax.axis_index("gx") % 2]).astype(jnp.int32)
+    small = pltpu.CompilerParams(vmem_limit_bytes=VMEM_LIMIT)
     y_rows = 4 * nx + 4 * TERMS
-    x_low, x_high, y_low, y_high = pl.pallas_call(
+    faces = pl.pallas_call(
         faces_kernel,
         out_shape=(array(2 * SLAB, R), array(2 * SLAB, R), array(y_rows, R), array(y_rows, R)),
-        in_specs=[vmem, vmem],
+        in_specs=[smem, vmem, vmem],
         out_specs=(vmem,) * 4,
+        compiler_params=small,
         name="faces",
-    )(flat, coef)
-    up_x = [(i, i + 1) for i in range(count_x - 1)]
-    up_y = [(i, i + 1) for i in range(count_y - 1)]
-    from_left = lax.ppermute(x_high, "gx", up_x)
-    from_right = lax.ppermute(x_low, "gx", [(b, a) for a, b in up_x])
-    from_below = lax.ppermute(y_high, "gy", up_y)
-    from_above = lax.ppermute(y_low, "gy", [(b, a) for a, b in up_y])
-
-    me = (lax.axis_index("gy") % 2).astype(jnp.int32).reshape(1)
+    )(me, flat, coef)
+
+    def swaps(first, count):
+        pairs = [(i, i + 1) for i in range(first, count - 1, 2)]
+        return pairs + [(b, a) for a, b in pairs]
+
+    halos = [
+        lax.ppermute(face, axis, swaps(first, count))
+        for face, axis, first, count in zip(faces, ("gx", "gx", "gy", "gy"), (0, 1, 0, 1), (count_x, count_x, count_y, count_y))
+    ]
     groups = nx // 2
+    turned = pl.pallas_call(
+        turn_kernel,
+        out_shape=array(groups, R, R),
+        in_specs=[vmem],
+        out_specs=vmem,
+        compiler_params=small,
+        name="turn",
+    )(flat)
+
     mine, other, raw_nominal = pl.pallas_call(
         images_kernel,
         out_shape=(array(HALF, R), array(HALF, R), array(nx * SLAB, R)),
-        in_specs=[smem, smem] + [vmem] * 6,
+        grid=(1,),
+        in_specs=[smem, smem, vmem]
+        + [pl.BlockSpec((SLAB, R), lambda i, at=at: (at, 0)) for at in (groups - 1, groups)]
+        + [vmem] * 5,
         out_specs=(vmem,) * 3,
         scratch_shapes=[
-            pltpu.VMEM((groups + 2, R, R), f32),
+            pltpu.VMEM((2 * SLAB, R), f32),
+            pltpu.VMEM((2 * SLAB, R), f32),
+            pltpu.VMEM((y_rows, R), f32),
+            pltpu.VMEM((y_rows, R), f32),
+            pltpu.VMEM((2, R, R), f32),
             pltpu.VMEM((R, 4 * nx), f32),
             pltpu.VMEM((R, 4 * nx), f32),
             pltpu.VMEM((6, TERMS, groups, R), f32),
@@ -412,8 +462,9 @@
             pltpu.VMEM((TERMS + 1, R, R), f32),
             pltpu.VMEM((R, R), f32),
         ],
+        compiler_params=small,
         name="images",
-    )(me, nominal_weights, flat, coef, from_left, from_right, from_below, from_above)
+    )(me, nominal_weights, turned, flat, flat, coef, *halos)
 
     swap = [(i, i ^ 1) for i in range(count_y)]
     along_z = [list(range(core, count_y, 2)) for core in range(2)]
@@ -434,6 +485,7 @@
         in_specs=[pl.BlockSpec((R, R), lambda i: (0, 0))],
         out_specs=pl.BlockSpec((R, R), lambda i: (0, 0)),
         scratch_shapes=[pltpu.VMEM((R, R), f32)],
+        compiler_params=small,
         name="factor",
     )(mine)
     ortho, nominal, reduced_ops, residual_grams = pl.pallas_call(
@@ -442,6 +494,7 @@
         in_specs=[smem] + [vmem] * 5,
         out_specs=(vmem,) * 4,
         scratch_shapes=[pltpu.VMEM((2 * HALF, R), f32)],
+        compiler_params=small,
         name="finish",
     )(me, mine, other, flat, raw_nominal, inverse_t)
     shape = raw_basis.shape

time: 96.6 us -> 84.5 us (0.87)
  Pallas kernels: 24 us -> 18.6 us
  starting transfers between devices: 15.5 us -> 11.5 us
  waiting for transfers between devices: 5.85 us -> 3.11 us
    ppermute x4, starting transfers between devices: 11.3 us -> 7.19 us  [shards(): lax.ppermute(face, axis, swaps(first, count))]
    ppermute x4, waiting for transfers between devices: 3.91 us -> 1.39 us  [shards(): lax.ppermute(face, axis, swaps(first, count))]
    all_to_all x1, blocking collectives: 17 us -> 19.5 us  [summed(): shard = jnp.sum(lax.all_to_all(parts, 'gx', 0, 0), axis=0)]
    all_to_all x1, blocking collectives: 19.2 us -> 17 us  [summed(): lax.all_to_all(along, 'gy', 0, 0, axis_index_groups=groups)]
    pallas_call x1, Pallas kernels: 8.99 us -> 7.26 us  [shards(): pl.pallas_call(images_kernel, out_shape=(array(HALF, R), array(HALF, R),...]
    pallas_call x1, Pallas kernels: 6.08 us -> 4.62 us  [shards(): pl.pallas_call(factor, out_shape=array(R, R), grid=(1,), in_specs=[pl.Blo...]
    pallas_call x1, Pallas kernels: 2.04 us -> 0.73 us  [shards(): pl.pallas_call(faces_kernel, out_shape=(array(2 * SLAB, R), array(2 * SLA...]
    pallas_call x1, Pallas kernels: 6.91 us -> 5.66 us  [shards(): pl.pallas_call(finish, out_shape=(array(nx * SLAB, R), array(nx * SLAB, R...]
where the time goes in v3:
time: 84.5 us; the launch traced here: 84.1 us
  blocking collectives  47.9 us (57%)
  Pallas kernels  18.6 us (22%)
  starting transfers between devices  11.5 us (14%)
  waiting for transfers between devices  3.11 us (4%)
  local copies, waits for them, and re-layouts  2.18 us (3%)
    all_to_all x1, blocking collectives, summed(): shard = jnp.sum(lax.all_to_all(parts, 'gx', 0, 0), axis=0)  19.5 us
    all_to_all x1, blocking collectives, summed(): lax.all_to_all(along, 'gy', 0, 0, axis_index_groups=groups)  17 us
    all_to_all x1, blocking collectives, summed(): return lax.all_to_all(spread, 'gx', 0, 0).reshape(values.shape)  11.3 us
    pallas_call x1, Pallas kernels, shards(): pl.pallas_call(images_kernel, out_shape=(array(HALF, R), array(HALF, R),...  7.26 us
    ppermute x4, starting transfers between devices, shards(): lax.ppermute(face, axis, swaps(first, count))  7.19 us
    pallas_call x1, Pallas kernels, shards(): pl.pallas_call(finish, out_shape=(array(nx * SLAB, R), array(nx * SLAB, R...  5.66 us
    pallas_call x1, Pallas kernels, shards(): pl.pallas_call(factor, out_shape=array(R, R), grid=(1,), in_specs=[pl.Blo...  4.62 us
    ppermute x1, starting transfers between devices, shards(): other = lax.ppermute(mine, 'gy', swap)  4.2 us
  transfers between devices with their start and end apart: 6, of which 3 were waited for; matrix products, arithmetic and copies ran while one was open for 0% of the time, Pallas kernels for 6%

profile of v3, /device:TPU:1, one launch (start us, length us, event | category | flops | bytes accessed | tf_op | source)
XLA Modules:
  0.0 84.1 jit_solution(4566878725978256806)
XLA Ops:
  0.6 0.1 pad_add_fusion.me.refs_0_
  0.7 1.2 %copy-done = f32[32,16,4,128]{3,2,1,0:T(4,128)S(1)} copy-done((f32[32,16,4,128]{3,2,1,0:T(4,128)S(1)}, f32[32,16,4,128]{3,2,1,0:T(4,128)}, u32[]{:S(2)}) %copy-start) | copy-done | bytes 1048600
  2.0 0.9 %copy-done.2 = f32[4,32,16,4]{1,3,2,0:T(4,128)S(1)} copy-done((f32[4,32,16,4]{1,3,2,0:T(4,128)S(1)}, f32[4,32,16,4]{1,3,2,0:T(4,128)}, u32[]{:S(2)}) %copy-start.2) | copy-done | bytes 32792
  2.9 0.7 faces.1
  3.6 3.3 %collective-permute-start.2 = (f32[144,128]{1,0:T(8,128)S(1)}, f32[144,128]{1,0:T(8,128)S(1)}, u32[]{:S(2)}, u32[]{:S(2)}) collective-permute-start(f32[144,128]{1,0:T(8,128)S(1)} %get-tuple-element.17), channel_id=1, source_target_pairs={{0,1},{2,3},{4,5},{6,7},{8,9},{10,11},{12,13},{14,15},{1,0},{3,2},... | collective-permute-start | bytes 221192 | tf_op jit(solution)/shard_map/ppermute | solution.py:429
  6.9 1.9 %collective-permute-start.3 = (f32[144,128]{1,0:T(8,128)S(1)}, f32[144,128]{1,0:T(8,128)S(1)}, u32[]{:S(2)}, u32[]{:S(2)}) collective-permute-start(f32[144,128]{1,0:T(8,128)S(1)} %get-tuple-element.18), channel_id=1, source_target_pairs={{1,2},{3,4},{5,6},{7,8},{9,10},{11,12},{13,14},{2,1},{4,3},{6,5},{... | collective-permute-start | bytes 221192 | tf_op jit(solution)/shard_map/ppermute | solution.py:429
  8.8 1.2 %collective-permute-start = (f32[128,128]{1,0:T(8,128)S(1)}, f32[128,128]{1,0:T(8,128)S(1)}, u32[]{:S(2)}, u32[]{:S(2)}) collective-permute-start(f32[128,128]{1,0:T(8,128)S(1)} %get-tuple-element.15), channel_id=1, source_target_pairs={{0,16},{32,48},{64,80},{96,112},{128,144},{160,176},{192,208},{224... | collective-permute-start | bytes 196616 | tf_op jit(solution)/shard_map/ppermute | solution.py:429
  10.0 0.8 collective-permute-start.1
  10.8 0.3 turn.1.turned
  11.1 0.9 %collective-permute-done.x_first = f32[128,128]{1,0:T(8,128)S(1)} collective-permute-done((f32[128,128]{1,0:T(8,128)S(1)}, f32[128,128]{1,0:T(8,128)S(1)}, u32[]{:S(2)}, u32[]{:S(2)}) %collective-permute-start) | collective-permute-done | bytes 65568 | tf_op jit(solution)/shard_map/ppermute | solution.py:429
  12.0 0.0 collective-permute-done.1.x_second
  12.0 0.0 collective-permute-done.2.y_first
  12.0 0.5 collective-permute-done.3.y_second
  12.5 7.3 %images.1 = (f32[768,128]{1,0:T(8,128)S(1)}, f32[768,128]{1,0:T(8,128)S(1)}, f32[2048,128]{1,0:T(8,128)S(1)}) custom-call(s32[2]{0:T(128)S(1)} %pad_add_fusion.me.refs_0_, f32[4]{0:T(128)S(1)} %copy-done.4, f32[16,128,128]{2,1,0:T(8,128)S(1)} %turn.1.turned, f32[2048,128]{1,0:T(8,128)S(1)} %bitcast.12, f32[2048,128]{1,0:T(8,128)S(1)} %bitcast.13, ...), custom_call_target="tpu_custom_call" | custom-call | tf_op jit(solution)/shard_map/images/pallas_call | solution.py:442
  19.8 0.1 collective-permute-start.4
  19.9 1.7 %collective-permute-done.4 = f32[768,128]{1,0:T(8,128)S(1)} collective-permute-done((f32[768,128]{1,0:T(8,128)S(1)}, f32[768,128]{1,0:T(8,128)S(1)}, u32[]{:S(2)}, u32[]{:S(2)}) %collective-permute-start.4) | collective-permute-done | bytes 393248 | tf_op jit(solution)/shard_map/ppermute | solution.py:471
  21.7 19.5 %all_to_all.15 = f32[16,48,128]{2,1,0:T(8,128)S(1)} all-to-all(f32[16,48,128]{2,1,0:T(8,128)S(1)} %bitcast.20), channel_id=1, replica_groups=mesh['gx'=16,'gy'=16] {'gx'}, dimensions={0} | all-to-all | bytes 786432 | tf_op jit(solution)/shard_map/all_to_all | solution.py:392
  41.2 0.0 copy-start.1
  41.2 17.0 %all_to_all.16 = f32[8,48,128]{2,1,0:T(8,128)S(1)} all-to-all(f32[8,48,128]{2,1,0:T(8,128)S(1)} %broadcast_in_dim.4), channel_id=1, replica_groups={{0,2,4,6,8,10,12,14},{1,3,5,7,9,11,13,15},{16,18,20,22,24,26,28,30},{17..., dimensions={0} | all-to-all | bytes 393216 | tf_op jit(solution)/shard_map/all_to_all | solution.py:395
  58.3 11.3 %all_to_all.17 = f32[16,48,128]{2,1,0:T(8,128)S(1)} all-to-all(f32[16,48,128]{2,1,0:T(8,128)S(1)} %broadcast_in_dim.5), channel_id=1, replica_groups=mesh['gx'=16,'gy'=16] {'gx'}, dimensions={0} | all-to-all | bytes 786432 | tf_op jit(solution)/shard_map/all_to_all | solution.py:397
  69.6 4.2 %collective-permute-start.5 = (f32[768,128]{1,0:T(8,128)S(1)}, f32[768,128]{1,0:T(8,128)S(1)}, u32[]{:S(2)}, u32[]{:S(2)}) collective-permute-start(f32[768,128]{1,0:T(8,128)S(1)} %bitcast.15), channel_id=1, source_target_pairs={{0,1},{1,0},{2,3},{3,2},{4,5},{5,4},{6,7},{7,6},{8,9},{9,8},{10,11... | collective-permute-start | bytes 1179656 | tf_op jit(solution)/shard_map/ppermute | solution.py:473
  73.8 4.6 %factor.1.refs_5_ = f32[128,128]{1,0:T(8,128)S(1)} custom-call(f32[768,128]{1,0:T(8,128)S(1)} %bitcast.16), custom_call_target="tpu_custom_call" | custom-call | tf_op jit(solution)/shard_map/factor/pallas_call | solution.py:481
  78.5 0.0 collective-permute-done.5.refs_2_
  78.5 5.7 %finish.1 = (f32[2048,128]{1,0:T(8,128)}, f32[2048,128]{1,0:T(8,128)}, f32[4,128,128]{2,1,0:T(8,128)}, f32[10,128,128]{2,1,0:T(8,128)}) custom-call(s32[2]{0:T(128)S(1)} %pad_add_fusion.me.refs_0_, f32[768,128]{1,0:T(8,128)S(1)} %bitcast.17, f32[768,128]{1,0:T(8,128)S(1)} %collective-permute-done.5.refs_2_, f32[2048,128]{1,0:T(8,128)S(1)} %bitcast.14, ...), custom_call_target="tpu_custom_call" | custom-call | tf_op jit(solution)/shard_map/finish/pallas_call | solution.py:491
  (12 shorter events, 0.1 us)
Async XLA Ops:
  0.7 1.2 %copy-start = (f32[32,16,4,128]{3,2,1,0:T(4,128)S(1)}, f32[32,16,4,128]{3,2,1,0:T(4,128)}, u32[]{:S(2)}) copy-start(f32[32,16,4,128]{3,2,1,0:T(4,128)} %param.3) | copy-start | bytes 3145732
  1.9 0.9 %copy-start.2 = (f32[4,32,16,4]{1,3,2,0:T(4,128)S(1)}, f32[4,32,16,4]{1,3,2,0:T(4,128)}, u32[]{:S(2)}) copy-start(f32[4,32,16,4]{1,3,2,0:T(4,128)} %param.4) | copy-start | bytes 98308
  3.6 8.4 %collective-permute-start.2 = (f32[144,128]{1,0:T(8,128)S(1)}, f32[144,128]{1,0:T(8,128)S(1)}, u32[]{:S(2)}, u32[]{:S(2)}) collective-permute-start(f32[144,128]{1,0:T(8,128)S(1)} %get-tuple-element.17), channel_id=1, source_target_pairs={{0,1},{2,3},{4,5},{6,7},{8,9},{10,11},{12,13},{14,15},{1,0},{3,2},... | collective-permute-start | bytes 221192 | tf_op jit(solution)/shard_map/ppermute | solution.py:429
  6.9 5.7 %collective-permute-start.3 = (f32[144,128]{1,0:T(8,128)S(1)}, f32[144,128]{1,0:T(8,128)S(1)}, u32[]{:S(2)}, u32[]{:S(2)}) collective-permute-start(f32[144,128]{1,0:T(8,128)S(1)} %get-tuple-element.18), channel_id=1, source_target_pairs={{1,2},{3,4},{5,6},{7,8},{9,10},{11,12},{13,14},{2,1},{4,3},{6,5},{... | collective-permute-start | bytes 221192 | tf_op jit(solution)/shard_map/ppermute | solution.py:429
  8.8 3.2 %collective-permute-start = (f32[128,128]{1,0:T(8,128)S(1)}, f32[128,128]{1,0:T(8,128)S(1)}, u32[]{:S(2)}, u32[]{:S(2)}) collective-permute-start(f32[128,128]{1,0:T(8,128)S(1)} %get-tuple-element.15), channel_id=1, source_target_pairs={{0,16},{32,48},{64,80},{96,112},{128,144},{160,176},{192,208},{224... | collective-permute-start | bytes 196616 | tf_op jit(solution)/shard_map/ppermute | solution.py:429
  10.0 2.5 %copy-start.3 = (f32[4,32,16,4]{1,3,2,0:T(4,128)S(1)}, f32[4,32,16,4]{1,3,2,0:T(4,128)}, u32[]{:S(2)}) copy-start(f32[4,32,16,4]{1,3,2,0:T(4,128)} %param.4) | copy-start | bytes 98308
  10.0 2.5 %copy-start.4 = (f32[4]{0:T(128)S(1)}, f32[4]{0:T(128)}, u32[]{:S(2)}) copy-start(f32[4]{0:T(128)} %nominal_weights.1) | copy-start | bytes 52
  10.0 2.0 %collective-permute-start.1 = (f32[128,128]{1,0:T(8,128)S(1)}, f32[128,128]{1,0:T(8,128)S(1)}, u32[]{:S(2)}, u32[]{:S(2)}) collective-permute-start(f32[128,128]{1,0:T(8,128)S(1)} %get-tuple-element.16), channel_id=1, source_target_pairs={{16,32},{48,64},{80,96},{112,128},{144,160},{176,192},{208,224},{3... | collective-permute-start | bytes 196616 | tf_op jit(solution)/shard_map/ppermute | solution.py:429
  19.8 1.8 %collective-permute-start.4 = (f32[768,128]{1,0:T(8,128)S(1)}, f32[768,128]{1,0:T(8,128)S(1)}, u32[]{:S(2)}, u32[]{:S(2)}) collective-permute-start(f32[768,128]{1,0:T(8,128)S(1)} %get-tuple-element.20), channel_id=1, source_target_pairs={{0,1},{1,0},{2,3},{3,2},{4,5},{5,4},{6,7},{7,6},{8,9},{9,8},{10,11... | collective-permute-start | bytes 1179656 | tf_op jit(solution)/shard_map/ppermute | solution.py:471
  41.2 37.2 %copy-start.1 = (f32[32,16,4,128]{3,2,1,0:T(4,128)S(1)}, f32[32,16,4,128]{3,2,1,0:T(4,128)}, u32[]{:S(2)}) copy-start(f32[32,16,4,128]{3,2,1,0:T(4,128)} %param.3) | copy-start | bytes 3145732
  69.6 8.8 %collective-permute-start.5 = (f32[768,128]{1,0:T(8,128)S(1)}, f32[768,128]{1,0:T(8,128)S(1)}, u32[]{:S(2)}, u32[]{:S(2)}) collective-permute-start(f32[768,128]{1,0:T(8,128)S(1)} %bitcast.15), channel_id=1, source_target_pairs={{0,1},{1,0},{2,3},{3,2},{4,5},{5,4},{6,7},{7,6},{8,9},{9,8},{10,11... | collective-permute-start | bytes 1179656 | tf_op jit(solution)/shard_map/ppermute | solution.py:473

commit v4 on v3

--- a/solution.py
+++ b/solution.py
@@ -17,19 +17,31 @@
 SLAB = 64
 WIDTH = (TERMS + 1) * R
 BLOCK = 32
+STEP = 4
 VMEM_LIMIT = 24 * 2**20
 halves = (
     ([(0, k + 1) for k in range(TERMS)], [(a + 1, b + 1) for a, b in crossed_pairs[:3]]),
     ([(k + 1, k + 1) for k in range(TERMS)], [(a + 1, b + 1) for a, b in crossed_pairs[3:]]),
 )
 
-def faces_kernel(me, basis, coef, x_first, x_second, y_first, y_second):
+def faces_kernel(me, basis, coef_in, x_first, x_second, y_first, y_second, x_low, x_high, y_low, y_high, coef, sems):
     lane = lax.broadcasted_iota(jnp.int32, (SLAB, R), 1)
-    slabs = basis.shape[0] // SLAB
+    slabs = basis.shape[0]
+    copies = [
+        pltpu.make_async_copy(coef_in, coef, sems.at[0]),
+        pltpu.make_async_copy(basis.at[0], x_low, sems.at[1]),
+        pltpu.make_async_copy(basis.at[slabs - 1], x_high, sems.at[2]),
+        pltpu.make_async_copy(basis.at[:, pl.ds(0, 8)], y_low, sems.at[3]),
+        pltpu.make_async_copy(basis.at[:, pl.ds(SLAB - 8, 8)], y_high, sems.at[4]),
+    ]
+    for copy in copies:
+        copy.start()
+    for copy in copies:
+        copy.wait()
 
     def x_faces(low, high):
-        low[0:SLAB, :] = basis[0:SLAB, :]
-        high[0:SLAB, :] = basis[(slabs - 1) * SLAB : slabs * SLAB, :]
+        low[0:SLAB, :] = x_low[...]
+        high[0:SLAB, :] = x_high[...]
         first = jnp.zeros((SLAB, R), f32)
         last = jnp.zeros((SLAB, R), f32)
         for k in range(TERMS):
@@ -41,8 +53,8 @@
 
     def y_faces(low, high):
         for x in range(slabs):
-            low[4 * x : 4 * x + 4, :] = basis[x * SLAB : x * SLAB + 4, :]
-            high[4 * x : 4 * x + 4, :] = basis[x * SLAB + SLAB - 4 : (x + 1) * SLAB, :]
+            low[4 * x : 4 * x + 4, :] = y_low[x, 0:4, :]
+            high[4 * x : 4 * x + 4, :] = y_high[x, 4:8, :]
         low[4 * slabs :, :] = jnp.zeros((16, R), f32)
         high[4 * slabs :, :] = jnp.zeros((16, R), f32)
         for k in range(TERMS):
@@ -134,8 +146,8 @@
     depth = lane % 4
 
     def images(chunk, slot):
-        for s in range(2):
-            j = 2 * chunk + s
+        for s in range(STEP):
+            j = STEP * chunk + s
             weights = [[face[f, k, j : j + 1, :] for f in range(6)] for k in range(TERMS)]
             for start in range(0, R, BLOCK):
                 rows = slice(start, start + BLOCK)
@@ -189,7 +201,7 @@
             else:
                 product[0:rows, start : start + 256] += value
 
-    chunks = groups // 2
+    chunks = groups // STEP
     for chunk in range(chunks):
         images(chunk, chunk % 2)
         if chunk > 0:
@@ -332,7 +344,8 @@
 
 
 def finish_kernel(
-    me, mine, other, basis, nominal, inverse_t, ortho_out, nominal_out, reduced_out, residual_out, packed, *, cells
+    me, mine, other, basis, nominal, inverse_t, ortho_hbm, nominal_hbm, reduced_hbm, residual_hbm,
+    packed, ortho_out, nominal_out, reduced_out, residual_out, stage, sems, *, cells
 ):
     packed[pl.ds(pl.multiple_of(me[0] * HALF, R), HALF), :] = mine[...]
     packed[pl.ds(pl.multiple_of((1 - me[0]) * HALF, R), HALF), :] = other[...]
@@ -352,18 +365,22 @@
         end = jnp.dot(jnp.concatenate([three, one], axis=1), last, preferred_element_type=f32)
         return out[:, :R] + (out[:, R:] + end)
 
+    copies = []
+
+    def send(source, target):
+        copies.append(pltpu.make_async_copy(source, target, sems.at[len(copies)]))
+        copies[-1].start()
+
     step = 512
-    for source, target in ((basis, ortho_out), (nominal, nominal_out)):
+    for source, target, away in ((basis, ortho_out, ortho_hbm), (nominal, nominal_out, nominal_hbm)):
         for start in range(0, basis.shape[0], step):
             target[start : start + step, :] = short(source[start : start + step, :])
+        send(target, away)
 
     r = lax.broadcasted_iota(jnp.int32, (R, R), 0)
     c = lax.broadcasted_iota(jnp.int32, (R, R), 1)
     scale = 1.0 / cells
-
-    def moved(matrix):
-        return product(product(matrix * scale).T)
-
+    places = []
     for h, (even, full) in enumerate(halves):
         tiles = [packed[h * HALF + q * R : h * HALF + (q + 1) * R, :] for q in range(HALF_SLOTS)]
         turned = [tile.T for tile in tiles[:3]]
@@ -379,10 +396,19 @@
             jnp.where(c >= r, tiles[2], turned[2]),
         ] + tiles[3:]
         for (a, b), matrix in zip(even + full, matrices):
-            if a == 0:
-                reduced_out[b - 1] = moved(matrix)
-            else:
-                residual_out[operator_pairs.index((a - 1, b - 1))] = moved(matrix)
+            at = len(places) * R
+            stage[at : at + R, :] = matrix * scale
+            places.append((reduced_out, b - 1) if a == 0 else (residual_out, operator_pairs.index((a - 1, b - 1))))
+    moved = product(stage[...])
+    for at in range(len(places)):
+        stage[at * R : (at + 1) * R, :] = moved[at * R : (at + 1) * R, :].T
+    moved = product(stage[...])
+    for at, (target, index) in enumerate(places):
+        target[index] = moved[at * R : (at + 1) * R, :]
+    send(reduced_out, reduced_hbm)
+    send(residual_out, residual_hbm)
+    for copy in copies:
+        copy.wait()
 
 
 def summed(values, groups):
@@ -405,6 +431,7 @@
     coef = jnp.transpose(coefficients, (0, 2, 3, 1)).reshape(-1, nx)
     vmem = pl.BlockSpec(memory_space=pltpu.VMEM)
     smem = pl.BlockSpec(memory_space=pltpu.SMEM)
+    hbm = pl.BlockSpec(memory_space=pltpu.HBM)
 
     def array(*shape):
         return jax.ShapeDtypeStruct(shape, f32)
@@ -415,11 +442,23 @@
     faces = pl.pallas_call(
         faces_kernel,
         out_shape=(array(2 * SLAB, R), array(2 * SLAB, R), array(y_rows, R), array(y_rows, R)),
-        in_specs=[smem, vmem, vmem],
+        in_specs=[smem, hbm, hbm],
         out_specs=(vmem,) * 4,
+        scratch_shapes=[
+            pltpu.VMEM((SLAB, R), f32),
+            pltpu.VMEM((SLAB, R), f32),
+            pltpu.VMEM((nx, 8, R), f32),
+            pltpu.VMEM((nx, 8, R), f32),
+            pltpu.VMEM(coef.shape, f32),
+            pltpu.SemaphoreType.DMA((5,)),
+        ],
         compiler_params=small,
         name="faces",
-    )(me, flat, coef)
+    )(
+        me,
+        pltpu.with_memory_space_constraint(flat.reshape(nx, SLAB, width), pltpu.HBM),
+        pltpu.with_memory_space_constraint(coef, pltpu.HBM),
+    )
 
     def swaps(first, count):
         pairs = [(i, i + 1) for i in range(first, count - 1, 2)]
@@ -456,8 +495,8 @@
             pltpu.VMEM((R, 4 * nx), f32),
             pltpu.VMEM((R, 4 * nx), f32),
             pltpu.VMEM((6, TERMS, groups, R), f32),
-            pltpu.VMEM((2, WIDTH, 2 * R), bf16),
-            pltpu.VMEM((2, WIDTH, 2 * R), bf16),
+            pltpu.VMEM((2, WIDTH, STEP * R), bf16),
+            pltpu.VMEM((2, WIDTH, STEP * R), bf16),
             pltpu.VMEM((WIDTH, 2 * WIDTH), f32),
             pltpu.VMEM((TERMS + 1, R, R), f32),
             pltpu.VMEM((R, R), f32),
@@ -492,8 +531,16 @@
         finish,
         out_shape=(array(nx * SLAB, R), array(nx * SLAB, R), array(TERMS, R, R), array(len(operator_pairs), R, R)),
         in_specs=[smem] + [vmem] * 5,
-        out_specs=(vmem,) * 4,
-        scratch_shapes=[pltpu.VMEM((2 * HALF, R), f32)],
+        out_specs=(hbm,) * 4,
+        scratch_shapes=[
+            pltpu.VMEM((2 * HALF, R), f32),
+            pltpu.VMEM((nx * SLAB, R), f32),
+            pltpu.VMEM((nx * SLAB, R), f32),
+            pltpu.VMEM((TERMS, R, R), f32),
+            pltpu.VMEM((len(operator_pairs), R, R), f32),
+            pltpu.VMEM(((TERMS + len(operator_pairs)) * R, R), f32),
+            pltpu.SemaphoreType.DMA((4,)),
+        ],
         compiler_params=small,
         name="finish",
     )(me, mine, other, flat, raw_nominal, inverse_t)

time: 84.5 us -> 80.4 us (0.951)
  local copies, waits for them, and re-layouts: 2.18 us -> 0.06 us
  Pallas kernels: 18.6 us -> 16.9 us
    pallas_call x1, Pallas kernels: 5.66 us -> 3.13 us  [shards(): pl.pallas_call(finish, out_shape=(array(nx * SLAB, R), array(nx * SLAB, R...]
    unnamed x10 -> x6, local copies, waits for them, and re-layouts: 2.14 us -> 0.02 us
    pallas_call x1, Pallas kernels: 0.73 us -> 1.84 us  [shards(): pl.pallas_call(faces_kernel, out_shape=(array(2 * SLAB, R), array(2 * SLA...]
where the time goes in v4:
time: 80.4 us; the launch traced here: 80.2 us
  blocking collectives  47.6 us (59%)
  Pallas kernels  16.9 us (21%)
  starting transfers between devices  11.3 us (14%)
  waiting for transfers between devices  3.22 us (4%)
  between operations  0.92 us (1%)
    all_to_all x1, blocking collectives, summed(): shard = jnp.sum(lax.all_to_all(parts, 'gx', 0, 0), axis=0)  19.4 us
    all_to_all x1, blocking collectives, summed(): lax.all_to_all(along, 'gy', 0, 0, axis_index_groups=groups)  16.9 us
    all_to_all x1, blocking collectives, summed(): return lax.all_to_all(spread, 'gx', 0, 0).reshape(values.shape)  11.3 us
    ppermute x4, starting transfers between devices, shards(): lax.ppermute(face, axis, swaps(first, count))  7.05 us
    pallas_call x1, Pallas kernels, shards(): pl.pallas_call(images_kernel, out_shape=(array(HALF, R), array(HALF, R),...  6.96 us
    pallas_call x1, Pallas kernels, shards(): pl.pallas_call(factor, out_shape=array(R, R), grid=(1,), in_specs=[pl.Blo...  4.62 us
    ppermute x1, starting transfers between devices, shards(): other = lax.ppermute(mine, 'gy', swap)  4.2 us
    pallas_call x1, Pallas kernels, shards(): pl.pallas_call(finish, out_shape=(array(nx * SLAB, R), array(nx * SLAB, R...  3.13 us
  transfers between devices with their start and end apart: 6, of which 3 were waited for; matrix products, arithmetic and copies ran while one was open for 0% of the time, Pallas kernels for 6%

profile of v4, /device:TPU:1, one launch (start us, length us, event | category | flops | bytes accessed | tf_op | source)
XLA Modules:
  0.0 80.2 jit_solution(12344255686982096998)
XLA Ops:
  0.6 0.0 copy-start
  0.7 0.1 pad_add_fusion.me.refs_0_
  0.7 1.8 %faces.1 = (f32[128,128]{1,0:T(8,128)S(1)}, f32[128,128]{1,0:T(8,128)S(1)}, f32[144,128]{1,0:T(8,128)S(1)}, f32[144,128]{1,0:T(8,128)S(1)}) custom-call(s32[2]{0:T(128)S(1)} %pad_add_fusion.me.refs_0_, f32[32,64,128]{2,1,0:T(8,128)} %bitcast.11, f32[256,32]{1,0:T(8,128)} %bitcast.19), custom_call_target="tpu_custom_call" | custom-call | tf_op jit(solution)/shard_map/faces/pallas_call | solution.py:442
  2.6 3.3 %collective-permute-start.2 = (f32[144,128]{1,0:T(8,128)S(1)}, f32[144,128]{1,0:T(8,128)S(1)}, u32[]{:S(2)}, u32[]{:S(2)}) collective-permute-start(f32[144,128]{1,0:T(8,128)S(1)} %get-tuple-element.17), channel_id=1, source_target_pairs={{0,1},{2,3},{4,5},{6,7},{8,9},{10,11},{12,13},{14,15},{1,0},{3,2},... | collective-permute-start | bytes 221192 | tf_op jit(solution)/shard_map/ppermute | solution.py:468
  5.9 1.9 %collective-permute-start.3 = (f32[144,128]{1,0:T(8,128)S(1)}, f32[144,128]{1,0:T(8,128)S(1)}, u32[]{:S(2)}, u32[]{:S(2)}) collective-permute-start(f32[144,128]{1,0:T(8,128)S(1)} %get-tuple-element.18), channel_id=1, source_target_pairs={{1,2},{3,4},{5,6},{7,8},{9,10},{11,12},{13,14},{2,1},{4,3},{6,5},{... | collective-permute-start | bytes 221192 | tf_op jit(solution)/shard_map/ppermute | solution.py:468
  7.8 1.2 %collective-permute-start = (f32[128,128]{1,0:T(8,128)S(1)}, f32[128,128]{1,0:T(8,128)S(1)}, u32[]{:S(2)}, u32[]{:S(2)}) collective-permute-start(f32[128,128]{1,0:T(8,128)S(1)} %get-tuple-element.15), channel_id=1, source_target_pairs={{0,16},{32,48},{64,80},{96,112},{128,144},{160,176},{192,208},{224... | collective-permute-start | bytes 196616 | tf_op jit(solution)/shard_map/ppermute | solution.py:468
  9.0 0.7 collective-permute-start.1
  9.7 0.0 copy-start.1
  9.7 0.0 copy-start.2
  9.7 0.3 turn.1.turned
  10.0 1.0 %collective-permute-done.x_first = f32[128,128]{1,0:T(8,128)S(1)} collective-permute-done((f32[128,128]{1,0:T(8,128)S(1)}, f32[128,128]{1,0:T(8,128)S(1)}, u32[]{:S(2)}, u32[]{:S(2)}) %collective-permute-start) | collective-permute-done | bytes 65568 | tf_op jit(solution)/shard_map/ppermute | solution.py:468
  11.0 0.0 collective-permute-done.1.x_second
  11.0 0.0 collective-permute-done.2.y_first
  11.0 0.5 collective-permute-done.3.y_second
  11.5 7.0 %images.1 = (f32[768,128]{1,0:T(8,128)S(1)}, f32[768,128]{1,0:T(8,128)S(1)}, f32[2048,128]{1,0:T(8,128)S(1)}) custom-call(s32[2]{0:T(128)S(1)} %pad_add_fusion.me.refs_0_, f32[4]{0:T(128)S(1)} %copy-done.2, f32[16,128,128]{2,1,0:T(8,128)S(1)} %turn.1.turned, f32[2048,128]{1,0:T(8,128)S(1)} %bitcast.13, f32[2048,128]{1,0:T(8,128)S(1)} %bitcast.14, ...), custom_call_target="tpu_custom_call" | custom-call | tf_op jit(solution)/shard_map/images/pallas_call | solution.py:481
  18.5 0.1 collective-permute-start.4
  18.6 1.7 %collective-permute-done.4 = f32[768,128]{1,0:T(8,128)S(1)} collective-permute-done((f32[768,128]{1,0:T(8,128)S(1)}, f32[768,128]{1,0:T(8,128)S(1)}, u32[]{:S(2)}, u32[]{:S(2)}) %collective-permute-start.4) | collective-permute-done | bytes 393248 | tf_op jit(solution)/shard_map/ppermute | solution.py:510
  20.4 19.4 %all_to_all.15 = f32[16,48,128]{2,1,0:T(8,128)S(1)} all-to-all(f32[16,48,128]{2,1,0:T(8,128)S(1)} %bitcast.21), channel_id=1, replica_groups=mesh['gx'=16,'gy'=16] {'gx'}, dimensions={0} | all-to-all | bytes 786432 | tf_op jit(solution)/shard_map/all_to_all | solution.py:418
  39.8 16.9 %all_to_all.16 = f32[8,48,128]{2,1,0:T(8,128)S(1)} all-to-all(f32[8,48,128]{2,1,0:T(8,128)S(1)} %broadcast_in_dim.4), channel_id=1, replica_groups={{0,2,4,6,8,10,12,14},{1,3,5,7,9,11,13,15},{16,18,20,22,24,26,28,30},{17..., dimensions={0} | all-to-all | bytes 393216 | tf_op jit(solution)/shard_map/all_to_all | solution.py:421
  56.7 11.3 %all_to_all.17 = f32[16,48,128]{2,1,0:T(8,128)S(1)} all-to-all(f32[16,48,128]{2,1,0:T(8,128)S(1)} %broadcast_in_dim.5), channel_id=1, replica_groups=mesh['gx'=16,'gy'=16] {'gx'}, dimensions={0} | all-to-all | bytes 786432 | tf_op jit(solution)/shard_map/all_to_all | solution.py:423
  68.1 4.2 %collective-permute-start.5 = (f32[768,128]{1,0:T(8,128)S(1)}, f32[768,128]{1,0:T(8,128)S(1)}, u32[]{:S(2)}, u32[]{:S(2)}) collective-permute-start(f32[768,128]{1,0:T(8,128)S(1)} %bitcast.16), channel_id=1, source_target_pairs={{0,1},{1,0},{2,3},{3,2},{4,5},{5,4},{6,7},{7,6},{8,9},{9,8},{10,11... | collective-permute-start | bytes 1179656 | tf_op jit(solution)/shard_map/ppermute | solution.py:512
  72.3 4.6 %factor.1.refs_5_ = f32[128,128]{1,0:T(8,128)S(1)} custom-call(f32[768,128]{1,0:T(8,128)S(1)} %bitcast.17), custom_call_target="tpu_custom_call" | custom-call | tf_op jit(solution)/shard_map/factor/pallas_call | solution.py:520
  76.9 0.0 collective-permute-done.5.refs_2_
  76.9 3.1 %finish.1 = (f32[2048,128]{1,0:T(8,128)}, f32[2048,128]{1,0:T(8,128)}, f32[4,128,128]{2,1,0:T(8,128)}, f32[10,128,128]{2,1,0:T(8,128)}) custom-call(s32[2]{0:T(128)S(1)} %pad_add_fusion.me.refs_0_, f32[768,128]{1,0:T(8,128)S(1)} %bitcast.18, f32[768,128]{1,0:T(8,128)S(1)} %collective-permute-done.5.refs_2_, f32[2048,128]{1,0:T(8,128)S(1)} %bitcast.15, ...), custom_call_target="tpu_custom_call" | custom-call | tf_op jit(solution)/shard_map/finish/pallas_call | solution.py:530
  (8 shorter events, 0.1 us)
Async XLA Ops:
  0.6 9.0 %copy-start = (f32[32,16,4,128]{3,2,1,0:T(4,128)S(1)}, f32[32,16,4,128]{3,2,1,0:T(4,128)}, u32[]{:S(2)}) copy-start(f32[32,16,4,128]{3,2,1,0:T(4,128)} %param.3) | copy-start | bytes 3145732
  2.6 8.4 %collective-permute-start.2 = (f32[144,128]{1,0:T(8,128)S(1)}, f32[144,128]{1,0:T(8,128)S(1)}, u32[]{:S(2)}, u32[]{:S(2)}) collective-permute-start(f32[144,128]{1,0:T(8,128)S(1)} %get-tuple-element.17), channel_id=1, source_target_pairs={{0,1},{2,3},{4,5},{6,7},{8,9},{10,11},{12,13},{14,15},{1,0},{3,2},... | collective-permute-start | bytes 221192 | tf_op jit(solution)/shard_map/ppermute | solution.py:468
  5.9 5.7 %collective-permute-start.3 = (f32[144,128]{1,0:T(8,128)S(1)}, f32[144,128]{1,0:T(8,128)S(1)}, u32[]{:S(2)}, u32[]{:S(2)}) collective-permute-start(f32[144,128]{1,0:T(8,128)S(1)} %get-tuple-element.18), channel_id=1, source_target_pairs={{1,2},{3,4},{5,6},{7,8},{9,10},{11,12},{13,14},{2,1},{4,3},{6,5},{... | collective-permute-start | bytes 221192 | tf_op jit(solution)/shard_map/ppermute | solution.py:468
  7.8 3.2 %collective-permute-start = (f32[128,128]{1,0:T(8,128)S(1)}, f32[128,128]{1,0:T(8,128)S(1)}, u32[]{:S(2)}, u32[]{:S(2)}) collective-permute-start(f32[128,128]{1,0:T(8,128)S(1)} %get-tuple-element.15), channel_id=1, source_target_pairs={{0,16},{32,48},{64,80},{96,112},{128,144},{160,176},{192,208},{224... | collective-permute-start | bytes 196616 | tf_op jit(solution)/shard_map/ppermute | solution.py:468
  9.0 2.0 %collective-permute-start.1 = (f32[128,128]{1,0:T(8,128)S(1)}, f32[128,128]{1,0:T(8,128)S(1)}, u32[]{:S(2)}, u32[]{:S(2)}) collective-permute-start(f32[128,128]{1,0:T(8,128)S(1)} %get-tuple-element.16), channel_id=1, source_target_pairs={{16,32},{48,64},{80,96},{112,128},{144,160},{176,192},{208,224},{3... | collective-permute-start | bytes 196616 | tf_op jit(solution)/shard_map/ppermute | solution.py:468
  9.7 1.9 %copy-start.1 = (f32[4,32,16,4]{1,3,2,0:T(4,128)S(1)}, f32[4,32,16,4]{1,3,2,0:T(4,128)}, u32[]{:S(2)}) copy-start(f32[4,32,16,4]{1,3,2,0:T(4,128)} %param.4) | copy-start | bytes 98308
  9.7 1.9 %copy-start.2 = (f32[4]{0:T(128)S(1)}, f32[4]{0:T(128)}, u32[]{:S(2)}) copy-start(f32[4]{0:T(128)} %nominal_weights.1) | copy-start | bytes 52
  18.5 1.8 %collective-permute-start.4 = (f32[768,128]{1,0:T(8,128)S(1)}, f32[768,128]{1,0:T(8,128)S(1)}, u32[]{:S(2)}, u32[]{:S(2)}) collective-permute-start(f32[768,128]{1,0:T(8,128)S(1)} %get-tuple-element.20), channel_id=1, source_target_pairs={{0,1},{1,0},{2,3},{3,2},{4,5},{5,4},{6,7},{7,6},{8,9},{9,8},{10,11... | collective-permute-start | bytes 1179656 | tf_op jit(solution)/shard_map/ppermute | solution.py:510
  68.1 8.8 %collective-permute-start.5 = (f32[768,128]{1,0:T(8,128)S(1)}, f32[768,128]{1,0:T(8,128)S(1)}, u32[]{:S(2)}, u32[]{:S(2)}) collective-permute-start(f32[768,128]{1,0:T(8,128)S(1)} %bitcast.16), channel_id=1, source_target_pairs={{0,1},{1,0},{2,3},{3,2},{4,5},{5,4},{6,7},{7,6},{8,9},{9,8},{10,11... | collective-permute-start | bytes 1179656 | tf_op jit(solution)/shard_map/ppermute | solution.py:512

commit v5 on v4

--- a/solution.py
+++ b/solution.py
@@ -23,6 +23,7 @@
     ([(0, k + 1) for k in range(TERMS)], [(a + 1, b + 1) for a, b in crossed_pairs[:3]]),
     ([(k + 1, k + 1) for k in range(TERMS)], [(a + 1, b + 1) for a, b in crossed_pairs[3:]]),
 )
+
 
 def faces_kernel(me, basis, coef_in, x_first, x_second, y_first, y_second, x_low, x_high, y_low, y_high, coef, sems):
     lane = lax.broadcasted_iota(jnp.int32, (SLAB, R), 1)
@@ -464,10 +465,9 @@
         pairs = [(i, i + 1) for i in range(first, count - 1, 2)]
         return pairs + [(b, a) for a, b in pairs]
 
-    halos = [
-        lax.ppermute(face, axis, swaps(first, count))
-        for face, axis, first, count in zip(faces, ("gx", "gx", "gy", "gy"), (0, 1, 0, 1), (count_x, count_x, count_y, count_y))
-    ]
+    halos = []
+    for face, axis, first in zip(faces, ("gx", "gx", "gy", "gy"), (0, 1, 0, 1)):
+        halos.append(lax.ppermute(face, axis, swaps(first, lax.axis_size(axis))))
     groups = nx // 2
     turned = pl.pallas_call(
         turn_kernel,

time: 80.4 us -> 80.4 us (level)
  no operation moved by 1% of the time
where the time goes in v5:
time: 80.4 us; the launch traced here: 80.2 us
  blocking collectives  47.6 us (59%)
  Pallas kernels  16.9 us (21%)
  starting transfers between devices  11.3 us (14%)
  waiting for transfers between devices  3.22 us (4%)
  between operations  0.92 us (1%)
    all_to_all x1, blocking collectives, summed(): shard = jnp.sum(lax.all_to_all(parts, 'gx', 0, 0), axis=0)  19.4 us
    all_to_all x1, blocking collectives, summed(): lax.all_to_all(along, 'gy', 0, 0, axis_index_groups=groups)  16.9 us
    all_to_all x1, blocking collectives, summed(): return lax.all_to_all(spread, 'gx', 0, 0).reshape(values.shape)  11.3 us
    ppermute x4, starting transfers between devices, shards(): halos.append(lax.ppermute(face, axis, swaps(first, lax.axis_size(axis))))  7.05 us
    pallas_call x1, Pallas kernels, shards(): pl.pallas_call(images_kernel, out_shape=(array(HALF, R), array(HALF, R),...  6.96 us
    pallas_call x1, Pallas kernels, shards(): pl.pallas_call(factor, out_shape=array(R, R), grid=(1,), in_specs=[pl.Blo...  4.62 us
    ppermute x1, starting transfers between devices, shards(): other = lax.ppermute(mine, 'gy', swap)  4.2 us
    pallas_call x1, Pallas kernels, shards(): pl.pallas_call(finish, out_shape=(array(nx * SLAB, R), array(nx * SLAB, R...  3.13 us
  transfers between devices with their start and end apart: 6, of which 3 were waited for; matrix products, arithmetic and copies ran while one was open for 0% of the time, Pallas kernels for 6%

profile of v5, /device:TPU:1, one launch (start us, length us, event | category | flops | bytes accessed | tf_op | source)
XLA Modules:
  0.0 80.2 jit_solution(12344255686982096998)
XLA Ops:
  0.6 0.0 copy-start
  0.7 0.1 pad_add_fusion.me.refs_0_
  0.7 1.8 %faces.1 = (f32[128,128]{1,0:T(8,128)S(1)}, f32[128,128]{1,0:T(8,128)S(1)}, f32[144,128]{1,0:T(8,128)S(1)}, f32[144,128]{1,0:T(8,128)S(1)}) custom-call(s32[2]{0:T(128)S(1)} %pad_add_fusion.me.refs_0_, f32[32,64,128]{2,1,0:T(8,128)} %bitcast.11, f32[256,32]{1,0:T(8,128)} %bitcast.19), custom_call_target="tpu_custom_call" | custom-call | tf_op jit(solution)/shard_map/faces/pallas_call | solution.py:443
  2.6 3.3 %collective-permute-start.2 = (f32[144,128]{1,0:T(8,128)S(1)}, f32[144,128]{1,0:T(8,128)S(1)}, u32[]{:S(2)}, u32[]{:S(2)}) collective-permute-start(f32[144,128]{1,0:T(8,128)S(1)} %get-tuple-element.17), channel_id=1, source_target_pairs={{0,1},{2,3},{4,5},{6,7},{8,9},{10,11},{12,13},{14,15},{1,0},{3,2},... | collective-permute-start | bytes 221192 | tf_op jit(solution)/shard_map/ppermute | solution.py:470
  5.9 1.9 %collective-permute-start.3 = (f32[144,128]{1,0:T(8,128)S(1)}, f32[144,128]{1,0:T(8,128)S(1)}, u32[]{:S(2)}, u32[]{:S(2)}) collective-permute-start(f32[144,128]{1,0:T(8,128)S(1)} %get-tuple-element.18), channel_id=1, source_target_pairs={{1,2},{3,4},{5,6},{7,8},{9,10},{11,12},{13,14},{2,1},{4,3},{6,5},{... | collective-permute-start | bytes 221192 | tf_op jit(solution)/shard_map/ppermute | solution.py:470
  7.8 1.2 %collective-permute-start = (f32[128,128]{1,0:T(8,128)S(1)}, f32[128,128]{1,0:T(8,128)S(1)}, u32[]{:S(2)}, u32[]{:S(2)}) collective-permute-start(f32[128,128]{1,0:T(8,128)S(1)} %get-tuple-element.15), channel_id=1, source_target_pairs={{0,16},{32,48},{64,80},{96,112},{128,144},{160,176},{192,208},{224... | collective-permute-start | bytes 196616 | tf_op jit(solution)/shard_map/ppermute | solution.py:470
  9.0 0.7 collective-permute-start.1
  9.7 0.0 copy-start.1
  9.7 0.0 copy-start.2
  9.7 0.3 turn.1.turned
  10.0 1.0 %collective-permute-done.x_first = f32[128,128]{1,0:T(8,128)S(1)} collective-permute-done((f32[128,128]{1,0:T(8,128)S(1)}, f32[128,128]{1,0:T(8,128)S(1)}, u32[]{:S(2)}, u32[]{:S(2)}) %collective-permute-start) | collective-permute-done | bytes 65568 | tf_op jit(solution)/shard_map/ppermute | solution.py:470
  11.0 0.0 collective-permute-done.1.x_second
  11.0 0.0 collective-permute-done.2.y_first
  11.0 0.5 collective-permute-done.3.y_second
  11.5 7.0 %images.1 = (f32[768,128]{1,0:T(8,128)S(1)}, f32[768,128]{1,0:T(8,128)S(1)}, f32[2048,128]{1,0:T(8,128)S(1)}) custom-call(s32[2]{0:T(128)S(1)} %pad_add_fusion.me.refs_0_, f32[4]{0:T(128)S(1)} %copy-done.2, f32[16,128,128]{2,1,0:T(8,128)S(1)} %turn.1.turned, f32[2048,128]{1,0:T(8,128)S(1)} %bitcast.13, f32[2048,128]{1,0:T(8,128)S(1)} %bitcast.14, ...), custom_call_target="tpu_custom_call" | custom-call | tf_op jit(solution)/shard_map/images/pallas_call | solution.py:481
  18.5 0.1 collective-permute-start.4
  18.6 1.7 %collective-permute-done.4 = f32[768,128]{1,0:T(8,128)S(1)} collective-permute-done((f32[768,128]{1,0:T(8,128)S(1)}, f32[768,128]{1,0:T(8,128)S(1)}, u32[]{:S(2)}, u32[]{:S(2)}) %collective-permute-start.4) | collective-permute-done | bytes 393248 | tf_op jit(solution)/shard_map/ppermute | solution.py:510
  20.4 19.4 %all_to_all.15 = f32[16,48,128]{2,1,0:T(8,128)S(1)} all-to-all(f32[16,48,128]{2,1,0:T(8,128)S(1)} %bitcast.21), channel_id=1, replica_groups=mesh['gx'=16,'gy'=16] {'gx'}, dimensions={0} | all-to-all | bytes 786432 | tf_op jit(solution)/shard_map/all_to_all | solution.py:419
  39.8 16.9 %all_to_all.16 = f32[8,48,128]{2,1,0:T(8,128)S(1)} all-to-all(f32[8,48,128]{2,1,0:T(8,128)S(1)} %broadcast_in_dim.4), channel_id=1, replica_groups={{0,2,4,6,8,10,12,14},{1,3,5,7,9,11,13,15},{16,18,20,22,24,26,28,30},{17..., dimensions={0} | all-to-all | bytes 393216 | tf_op jit(solution)/shard_map/all_to_all | solution.py:422
  56.7 11.3 %all_to_all.17 = f32[16,48,128]{2,1,0:T(8,128)S(1)} all-to-all(f32[16,48,128]{2,1,0:T(8,128)S(1)} %broadcast_in_dim.5), channel_id=1, replica_groups=mesh['gx'=16,'gy'=16] {'gx'}, dimensions={0} | all-to-all | bytes 786432 | tf_op jit(solution)/shard_map/all_to_all | solution.py:424
  68.1 4.2 %collective-permute-start.5 = (f32[768,128]{1,0:T(8,128)S(1)}, f32[768,128]{1,0:T(8,128)S(1)}, u32[]{:S(2)}, u32[]{:S(2)}) collective-permute-start(f32[768,128]{1,0:T(8,128)S(1)} %bitcast.16), channel_id=1, source_target_pairs={{0,1},{1,0},{2,3},{3,2},{4,5},{5,4},{6,7},{7,6},{8,9},{9,8},{10,11... | collective-permute-start | bytes 1179656 | tf_op jit(solution)/shard_map/ppermute | solution.py:512
  72.3 4.6 %factor.1.refs_5_ = f32[128,128]{1,0:T(8,128)S(1)} custom-call(f32[768,128]{1,0:T(8,128)S(1)} %bitcast.17), custom_call_target="tpu_custom_call" | custom-call | tf_op jit(solution)/shard_map/factor/pallas_call | solution.py:520
  76.9 0.0 collective-permute-done.5.refs_2_
  76.9 3.1 %finish.1 = (f32[2048,128]{1,0:T(8,128)}, f32[2048,128]{1,0:T(8,128)}, f32[4,128,128]{2,1,0:T(8,128)}, f32[10,128,128]{2,1,0:T(8,128)}) custom-call(s32[2]{0:T(128)S(1)} %pad_add_fusion.me.refs_0_, f32[768,128]{1,0:T(8,128)S(1)} %bitcast.18, f32[768,128]{1,0:T(8,128)S(1)} %collective-permute-done.5.refs_2_, f32[2048,128]{1,0:T(8,128)S(1)} %bitcast.15, ...), custom_call_target="tpu_custom_call" | custom-call | tf_op jit(solution)/shard_map/finish/pallas_call | solution.py:530
  (8 shorter events, 0.1 us)
Async XLA Ops:
  0.6 9.0 %copy-start = (f32[32,16,4,128]{3,2,1,0:T(4,128)S(1)}, f32[32,16,4,128]{3,2,1,0:T(4,128)}, u32[]{:S(2)}) copy-start(f32[32,16,4,128]{3,2,1,0:T(4,128)} %param.3) | copy-start | bytes 3145732
  2.6 8.4 %collective-permute-start.2 = (f32[144,128]{1,0:T(8,128)S(1)}, f32[144,128]{1,0:T(8,128)S(1)}, u32[]{:S(2)}, u32[]{:S(2)}) collective-permute-start(f32[144,128]{1,0:T(8,128)S(1)} %get-tuple-element.17), channel_id=1, source_target_pairs={{0,1},{2,3},{4,5},{6,7},{8,9},{10,11},{12,13},{14,15},{1,0},{3,2},... | collective-permute-start | bytes 221192 | tf_op jit(solution)/shard_map/ppermute | solution.py:470
  5.9 5.7 %collective-permute-start.3 = (f32[144,128]{1,0:T(8,128)S(1)}, f32[144,128]{1,0:T(8,128)S(1)}, u32[]{:S(2)}, u32[]{:S(2)}) collective-permute-start(f32[144,128]{1,0:T(8,128)S(1)} %get-tuple-element.18), channel_id=1, source_target_pairs={{1,2},{3,4},{5,6},{7,8},{9,10},{11,12},{13,14},{2,1},{4,3},{6,5},{... | collective-permute-start | bytes 221192 | tf_op jit(solution)/shard_map/ppermute | solution.py:470
  7.8 3.2 %collective-permute-start = (f32[128,128]{1,0:T(8,128)S(1)}, f32[128,128]{1,0:T(8,128)S(1)}, u32[]{:S(2)}, u32[]{:S(2)}) collective-permute-start(f32[128,128]{1,0:T(8,128)S(1)} %get-tuple-element.15), channel_id=1, source_target_pairs={{0,16},{32,48},{64,80},{96,112},{128,144},{160,176},{192,208},{224... | collective-permute-start | bytes 196616 | tf_op jit(solution)/shard_map/ppermute | solution.py:470
  9.0 2.0 %collective-permute-start.1 = (f32[128,128]{1,0:T(8,128)S(1)}, f32[128,128]{1,0:T(8,128)S(1)}, u32[]{:S(2)}, u32[]{:S(2)}) collective-permute-start(f32[128,128]{1,0:T(8,128)S(1)} %get-tuple-element.16), channel_id=1, source_target_pairs={{16,32},{48,64},{80,96},{112,128},{144,160},{176,192},{208,224},{3... | collective-permute-start | bytes 196616 | tf_op jit(solution)/shard_map/ppermute | solution.py:470
  9.7 1.9 %copy-start.1 = (f32[4,32,16,4]{1,3,2,0:T(4,128)S(1)}, f32[4,32,16,4]{1,3,2,0:T(4,128)}, u32[]{:S(2)}) copy-start(f32[4,32,16,4]{1,3,2,0:T(4,128)} %param.4) | copy-start | bytes 98308
  9.7 1.9 %copy-start.2 = (f32[4]{0:T(128)S(1)}, f32[4]{0:T(128)}, u32[]{:S(2)}) copy-start(f32[4]{0:T(128)} %nominal_weights.1) | copy-start | bytes 52
  18.5 1.8 %collective-permute-start.4 = (f32[768,128]{1,0:T(8,128)S(1)}, f32[768,128]{1,0:T(8,128)S(1)}, u32[]{:S(2)}, u32[]{:S(2)}) collective-permute-start(f32[768,128]{1,0:T(8,128)S(1)} %get-tuple-element.20), channel_id=1, source_target_pairs={{0,1},{1,0},{2,3},{3,2},{4,5},{5,4},{6,7},{7,6},{8,9},{9,8},{10,11... | collective-permute-start | bytes 1179656 | tf_op jit(solution)/shard_map/ppermute | solution.py:510
  68.1 8.8 %collective-permute-start.5 = (f32[768,128]{1,0:T(8,128)S(1)}, f32[768,128]{1,0:T(8,128)S(1)}, u32[]{:S(2)}, u32[]{:S(2)}) collective-permute-start(f32[768,128]{1,0:T(8,128)S(1)} %bitcast.16), channel_id=1, source_target_pairs={{0,1},{1,0},{2,3},{3,2},{4,5},{5,4},{6,7},{7,6},{8,9},{9,8},{10,11... | collective-permute-start | bytes 1179656 | tf_op jit(solution)/shard_map/ppermute | solution.py:512

commit v6 on v5

--- a/solution.py
+++ b/solution.py
@@ -23,6 +23,10 @@
     ([(0, k + 1) for k in range(TERMS)], [(a + 1, b + 1) for a, b in crossed_pairs[:3]]),
     ([(k + 1, k + 1) for k in range(TERMS)], [(a + 1, b + 1) for a, b in crossed_pairs[3:]]),
 )
+
+
+def flipped(tile):
+    return jnp.concatenate([tile, jnp.zeros((R - tile.shape[0], R), f32)], axis=0).T
 
 
 def faces_kernel(me, basis, coef_in, x_first, x_second, y_first, y_second, x_low, x_high, y_low, y_high, coef, sems):
@@ -43,14 +47,14 @@
     def x_faces(low, high):
         low[0:SLAB, :] = x_low[...]
         high[0:SLAB, :] = x_high[...]
-        first = jnp.zeros((SLAB, R), f32)
-        last = jnp.zeros((SLAB, R), f32)
+        both = jnp.zeros((SLAB, R), f32)
         for k in range(TERMS):
             rows = coef[k * SLAB : (k + 1) * SLAB, :]
-            first = jnp.where(lane == k, rows[:, 0:1], first)
-            last = jnp.where(lane == k, rows[:, slabs - 1 : slabs], last)
-        low[SLAB : 2 * SLAB, :] = first
-        high[SLAB : 2 * SLAB, :] = last
+            both = jnp.where(lane == k, rows[:, 0:1], both)
+            both = jnp.where(lane == k + TERMS, rows[:, slabs - 1 : slabs], both)
+        lines = flipped(both)[0 : 2 * TERMS]
+        low[SLAB:, :] = lines
+        high[SLAB:, :] = lines
 
     def y_faces(low, high):
         for x in range(slabs):
@@ -113,11 +117,8 @@
     def joined(rows):
         return jnp.where(first, rows[0:groups], pltpu.roll(rows[groups:slabs], SLAB, 1))
 
-    def flipped(tile):
-        return jnp.concatenate([tile, jnp.zeros((R - tile.shape[0], R), f32)], axis=0).T
-
-    left_coef = flipped(from_left[SLAB : 2 * SLAB, :])
-    right_coef = flipped(from_right[SLAB : 2 * SLAB, :])
+    left_coef = from_left[SLAB + TERMS : SLAB + 2 * TERMS, :]
+    right_coef = from_right[SLAB : SLAB + TERMS, :]
     above_coef = flipped(from_above[4 * slabs :, :])
     below_coef = flipped(from_below[4 * slabs :, :])
     for k in range(TERMS):
@@ -417,9 +418,10 @@
     width = values.shape[1]
     parts = values.reshape(count, -1, width)
     shard = jnp.sum(lax.all_to_all(parts, "gx", 0, 0), axis=0)
-    depth = len(groups[0])
-    along = jnp.broadcast_to(shard[None], (depth,) + shard.shape)
-    shard = jnp.sum(lax.all_to_all(along, "gy", 0, 0, axis_index_groups=groups), axis=0)
+    distance = len(groups)
+    while distance < lax.axis_size("gy"):
+        shard = shard + lax.ppermute(shard, "gy", [(i, i ^ distance) for i in range(lax.axis_size("gy"))])
+        distance *= 2
     spread = jnp.broadcast_to(shard[None], (count,) + shard.shape)
     return lax.all_to_all(spread, "gx", 0, 0).reshape(values.shape)
 
@@ -439,10 +441,10 @@
 
     me = jnp.stack([lax.axis_index("gy") % 2, lax.axis_index("gx") % 2]).astype(jnp.int32)
     small = pltpu.CompilerParams(vmem_limit_bytes=VMEM_LIMIT)
-    y_rows = 4 * nx + 4 * TERMS
+    x_rows, y_rows = SLAB + 2 * TERMS, 4 * nx + 4 * TERMS
     faces = pl.pallas_call(
         faces_kernel,
-        out_shape=(array(2 * SLAB, R), array(2 * SLAB, R), array(y_rows, R), array(y_rows, R)),
+        out_shape=(array(x_rows, R), array(x_rows, R), array(y_rows, R), array(y_rows, R)),
         in_specs=[smem, hbm, hbm],
         out_specs=(vmem,) * 4,
         scratch_shapes=[
@@ -487,8 +489,8 @@
         + [vmem] * 5,
         out_specs=(vmem,) * 3,
         scratch_shapes=[
-            pltpu.VMEM((2 * SLAB, R), f32),
-            pltpu.VMEM((2 * SLAB, R), f32),
+            pltpu.VMEM((x_rows, R), f32),
+            pltpu.VMEM((x_rows, R), f32),
             pltpu.VMEM((y_rows, R), f32),
             pltpu.VMEM((y_rows, R), f32),
             pltpu.VMEM((2, R, R), f32),

time: 80.4 us -> 79.7 us (level)
  blocking collectives: 47.6 us -> 30.6 us
  starting transfers between devices: 11.3 us -> 23.5 us
  waiting for transfers between devices: 3.22 us -> 7.4 us
    all_to_all x1 -> x0, blocking collectives: 16.9 us -> none  [summed(): lax.all_to_all(along, 'gy', 0, 0, axis_index_groups=groups)]
    ppermute x0 -> x3, starting transfers between devices: none -> 10.7 us  [summed(): lax.ppermute(shard, 'gy', [(i, i ^ distance) for i in range(lax.axis_size...]
    ppermute x0 -> x3, waiting for transfers between devices: none -> 4.2 us  [summed(): lax.ppermute(shard, 'gy', [(i, i ^ distance) for i in range(lax.axis_size...]
    ppermute x1, starting transfers between devices: 4.2 us -> 5.59 us  [shards(): other = lax.ppermute(mine, 'gy', swap)]
  transfers between devices with their start and end apart: 6 -> 9, of which waited for: 3 -> 6; matrix products, arithmetic and copies ran while one was open for 0% -> 0% of each run, Pallas kernels for 6% -> 6%
where the time goes in v6:
time: 79.7 us; the launch traced here: 79.5 us
  blocking collectives  30.6 us (38%)
  starting transfers between devices  23.5 us (29%)
  Pallas kernels  16.9 us (21%)
  waiting for transfers between devices  7.4 us (9%)
  between operations  0.91 us (1%)
    all_to_all x1, blocking collectives, summed(): shard = jnp.sum(lax.all_to_all(parts, 'gx', 0, 0), axis=0)  19.1 us
    all_to_all x1, blocking collectives, summed(): return lax.all_to_all(spread, 'gx', 0, 0).reshape(values.shape)  11.5 us
    ppermute x3, starting transfers between devices, summed(): lax.ppermute(shard, 'gy', [(i, i ^ distance) for i in range(lax.axis_size...  10.7 us
    ppermute x4, starting transfers between devices, shards(): halos.append(lax.ppermute(face, axis, swaps(first, lax.axis_size(axis))))  7.06 us
    pallas_call x1, Pallas kernels, shards(): pl.pallas_call(images_kernel, out_shape=(array(HALF, R), array(HALF, R),...  6.93 us
    ppermute x1, starting transfers between devices, shards(): other = lax.ppermute(mine, 'gy', swap)  5.59 us
    pallas_call x1, Pallas kernels, shards(): pl.pallas_call(factor, out_shape=array(R, R), grid=(1,), in_specs=[pl.Blo...  4.62 us
    ppermute x3, waiting for transfers between devices, summed(): lax.ppermute(shard, 'gy', [(i, i ^ distance) for i in range(lax.axis_size...  4.2 us
  transfers between devices with their start and end apart: 9, of which 6 were waited for; matrix products, arithmetic and copies ran while one was open for 0% of the time, Pallas kernels for 6%

profile of v6, /device:TPU:1, one launch (start us, length us, event | category | flops | bytes accessed | tf_op | source)
XLA Modules:
  0.0 79.5 jit_solution(1462544510484019697)
XLA Ops:
  0.7 0.1 pad_add_fusion.me.refs_0_
  0.7 1.9 %faces.1 = (f32[72,128]{1,0:T(8,128)S(1)}, f32[72,128]{1,0:T(8,128)S(1)}, f32[144,128]{1,0:T(8,128)S(1)}, f32[144,128]{1,0:T(8,128)S(1)}) custom-call(s32[2]{0:T(128)S(1)} %pad_add_fusion.me.refs_0_, f32[32,64,128]{2,1,0:T(8,128)} %bitcast.11, f32[256,32]{1,0:T(8,128)} %bitcast.19), custom_call_target="tpu_custom_call" | custom-call | tf_op jit(solution)/shard_map/faces/pallas_call | solution.py:445
  2.6 3.3 %collective-permute-start.2 = (f32[144,128]{1,0:T(8,128)S(1)}, f32[144,128]{1,0:T(8,128)S(1)}, u32[]{:S(2)}, u32[]{:S(2)}) collective-permute-start(f32[144,128]{1,0:T(8,128)S(1)} %get-tuple-element.17), channel_id=1, source_target_pairs={{0,1},{2,3},{4,5},{6,7},{8,9},{10,11},{12,13},{14,15},{1,0},{3,2},... | collective-permute-start | bytes 221192 | tf_op jit(solution)/shard_map/ppermute | solution.py:472
  5.9 1.9 %collective-permute-start.3 = (f32[144,128]{1,0:T(8,128)S(1)}, f32[144,128]{1,0:T(8,128)S(1)}, u32[]{:S(2)}, u32[]{:S(2)}) collective-permute-start(f32[144,128]{1,0:T(8,128)S(1)} %get-tuple-element.18), channel_id=1, source_target_pairs={{1,2},{3,4},{5,6},{7,8},{9,10},{11,12},{13,14},{2,1},{4,3},{6,5},{... | collective-permute-start | bytes 221192 | tf_op jit(solution)/shard_map/ppermute | solution.py:472
  7.8 1.2 %collective-permute-start = (f32[72,128]{1,0:T(8,128)S(1)}, f32[72,128]{1,0:T(8,128)S(1)}, u32[]{:S(2)}, u32[]{:S(2)}) collective-permute-start(f32[72,128]{1,0:T(8,128)S(1)} %get-tuple-element.15), channel_id=1, source_target_pairs={{0,16},{32,48},{64,80},{96,112},{128,144},{160,176},{192,208},{224... | collective-permute-start | bytes 110600 | tf_op jit(solution)/shard_map/ppermute | solution.py:472
  9.0 0.7 collective-permute-start.1
  9.7 0.3 turn.1.turned
  10.1 0.7 collective-permute-done.x_first
  10.7 0.8 %collective-permute-done.3.y_second = f32[144,128]{1,0:T(8,128)S(1)} collective-permute-done((f32[144,128]{1,0:T(8,128)S(1)}, f32[144,128]{1,0:T(8,128)S(1)}, u32[]{:S(2)}, u32[]{:S(2)}) %collective-permute-start.3) | collective-permute-done | bytes 73760 | tf_op jit(solution)/shard_map/ppermute | solution.py:472
  11.6 6.9 %images.1 = (f32[768,128]{1,0:T(8,128)S(1)}, f32[768,128]{1,0:T(8,128)S(1)}, f32[2048,128]{1,0:T(8,128)S(1)}) custom-call(s32[2]{0:T(128)S(1)} %pad_add_fusion.me.refs_0_, f32[4]{0:T(128)S(1)} %copy-done.2, f32[16,128,128]{2,1,0:T(8,128)S(1)} %turn.1.turned, f32[2048,128]{1,0:T(8,128)S(1)} %bitcast.13, f32[2048,128]{1,0:T(8,128)S(1)} %bitcast.14, ...), custom_call_target="tpu_custom_call" | custom-call | tf_op jit(solution)/shard_map/images/pallas_call | solution.py:483
  18.5 0.1 collective-permute-start.4
  18.6 1.7 %collective-permute-done.4 = f32[768,128]{1,0:T(8,128)S(1)} collective-permute-done((f32[768,128]{1,0:T(8,128)S(1)}, f32[768,128]{1,0:T(8,128)S(1)}, u32[]{:S(2)}, u32[]{:S(2)}) %collective-permute-start.4) | collective-permute-done | bytes 393248 | tf_op jit(solution)/shard_map/ppermute | solution.py:512
  20.3 0.1 add.21
  20.4 19.1 %all_to_all.10 = f32[16,48,128]{2,1,0:T(8,128)S(1)} all-to-all(f32[16,48,128]{2,1,0:T(8,128)S(1)} %bitcast.21), channel_id=1, replica_groups=mesh['gx'=16,'gy'=16] {'gx'}, dimensions={0} | all-to-all | bytes 786432 | tf_op jit(solution)/shard_map/all_to_all | solution.py:420
  39.5 1.7 %collective-permute-start.5 = (f32[48,128]{1,0:T(8,128)S(1)}, f32[48,128]{1,0:T(8,128)S(1)}, u32[]{:S(2)}, u32[]{:S(2)}) collective-permute-start(f32[48,128]{1,0:T(8,128)S(1)} %reduce_sum.9), channel_id=1, source_target_pairs={{0,2},{1,3},{2,0},{3,1},{4,6},{5,7},{6,4},{7,5},{8,10},{9,11},{10,... | collective-permute-start | bytes 73736 | tf_op jit(solution)/shard_map/ppermute | solution.py:423
  41.2 1.2 %collective-permute-done.5 = f32[48,128]{1,0:T(8,128)S(1)} collective-permute-done((f32[48,128]{1,0:T(8,128)S(1)}, f32[48,128]{1,0:T(8,128)S(1)}, u32[]{:S(2)}, u32[]{:S(2)}) %collective-permute-start.5) | collective-permute-done | bytes 24608 | tf_op jit(solution)/shard_map/ppermute | solution.py:423
  42.4 4.2 %collective-permute-start.6 = (f32[48,128]{1,0:T(8,128)S(1)}, f32[48,128]{1,0:T(8,128)S(1)}, u32[]{:S(2)}, u32[]{:S(2)}) collective-permute-start(f32[48,128]{1,0:T(8,128)S(1)} %add.22), channel_id=1, source_target_pairs={{0,4},{1,5},{2,6},{3,7},{4,0},{5,1},{6,2},{7,3},{8,12},{9,13},{10,... | collective-permute-start | bytes 73736 | tf_op jit(solution)/shard_map/ppermute | solution.py:423
  46.6 1.2 %collective-permute-done.6 = f32[48,128]{1,0:T(8,128)S(1)} collective-permute-done((f32[48,128]{1,0:T(8,128)S(1)}, f32[48,128]{1,0:T(8,128)S(1)}, u32[]{:S(2)}, u32[]{:S(2)}) %collective-permute-start.6) | collective-permute-done | bytes 24608 | tf_op jit(solution)/shard_map/ppermute | solution.py:423
  47.9 4.8 %collective-permute-start.7 = (f32[48,128]{1,0:T(8,128)S(1)}, f32[48,128]{1,0:T(8,128)S(1)}, u32[]{:S(2)}, u32[]{:S(2)}) collective-permute-start(f32[48,128]{1,0:T(8,128)S(1)} %add.23), channel_id=1, source_target_pairs={{0,8},{1,9},{2,10},{3,11},{4,12},{5,13},{6,14},{7,15},{8,0},{9,1},... | collective-permute-start | bytes 73736 | tf_op jit(solution)/shard_map/ppermute | solution.py:423
  52.7 1.8 %collective-permute-done.7 = f32[48,128]{1,0:T(8,128)S(1)} collective-permute-done((f32[48,128]{1,0:T(8,128)S(1)}, f32[48,128]{1,0:T(8,128)S(1)}, u32[]{:S(2)}, u32[]{:S(2)}) %collective-permute-start.7) | collective-permute-done | bytes 24608 | tf_op jit(solution)/shard_map/ppermute | solution.py:423
  54.5 11.5 %all_to_all.11 = f32[16,48,128]{2,1,0:T(8,128)S(1)} all-to-all(f32[16,48,128]{2,1,0:T(8,128)S(1)} %broadcast_in_dim.2), channel_id=1, replica_groups=mesh['gx'=16,'gy'=16] {'gx'}, dimensions={0} | all-to-all | bytes 786432 | tf_op jit(solution)/shard_map/all_to_all | solution.py:426
  66.0 5.6 %collective-permute-start.8 = (f32[768,128]{1,0:T(8,128)S(1)}, f32[768,128]{1,0:T(8,128)S(1)}, u32[]{:S(2)}, u32[]{:S(2)}) collective-permute-start(f32[768,128]{1,0:T(8,128)S(1)} %bitcast.16), channel_id=1, source_target_pairs={{0,1},{1,0},{2,3},{3,2},{4,5},{5,4},{6,7},{7,6},{8,9},{9,8},{10,11... | collective-permute-start | bytes 1179656 | tf_op jit(solution)/shard_map/ppermute | solution.py:514
  71.6 4.6 %factor.1.refs_5_ = f32[128,128]{1,0:T(8,128)S(1)} custom-call(f32[768,128]{1,0:T(8,128)S(1)} %bitcast.17), custom_call_target="tpu_custom_call" | custom-call | tf_op jit(solution)/shard_map/factor/pallas_call | solution.py:522
  76.2 3.1 %finish.1 = (f32[2048,128]{1,0:T(8,128)}, f32[2048,128]{1,0:T(8,128)}, f32[4,128,128]{2,1,0:T(8,128)}, f32[10,128,128]{2,1,0:T(8,128)}) custom-call(s32[2]{0:T(128)S(1)} %pad_add_fusion.me.refs_0_, f32[768,128]{1,0:T(8,128)S(1)} %bitcast.18, f32[768,128]{1,0:T(8,128)S(1)} %collective-permute-done.8.refs_2_, f32[2048,128]{1,0:T(8,128)S(1)} %bitcast.15, ...), custom_call_target="tpu_custom_call" | custom-call | tf_op jit(solution)/shard_map/finish/pallas_call | solution.py:532
  (14 shorter events, 0.1 us)
Async XLA Ops:
  0.6 9.1 %copy-start = (f32[32,16,4,128]{3,2,1,0:T(4,128)S(1)}, f32[32,16,4,128]{3,2,1,0:T(4,128)}, u32[]{:S(2)}) copy-start(f32[32,16,4,128]{3,2,1,0:T(4,128)} %param.3) | copy-start | bytes 3145732
  2.6 8.1 %collective-permute-start.2 = (f32[144,128]{1,0:T(8,128)S(1)}, f32[144,128]{1,0:T(8,128)S(1)}, u32[]{:S(2)}, u32[]{:S(2)}) collective-permute-start(f32[144,128]{1,0:T(8,128)S(1)} %get-tuple-element.17), channel_id=1, source_target_pairs={{0,1},{2,3},{4,5},{6,7},{8,9},{10,11},{12,13},{14,15},{1,0},{3,2},... | collective-permute-start | bytes 221192 | tf_op jit(solution)/shard_map/ppermute | solution.py:472
  5.9 5.7 %collective-permute-start.3 = (f32[144,128]{1,0:T(8,128)S(1)}, f32[144,128]{1,0:T(8,128)S(1)}, u32[]{:S(2)}, u32[]{:S(2)}) collective-permute-start(f32[144,128]{1,0:T(8,128)S(1)} %get-tuple-element.18), channel_id=1, source_target_pairs={{1,2},{3,4},{5,6},{7,8},{9,10},{11,12},{13,14},{2,1},{4,3},{6,5},{... | collective-permute-start | bytes 221192 | tf_op jit(solution)/shard_map/ppermute | solution.py:472
  7.8 2.9 %collective-permute-start = (f32[72,128]{1,0:T(8,128)S(1)}, f32[72,128]{1,0:T(8,128)S(1)}, u32[]{:S(2)}, u32[]{:S(2)}) collective-permute-start(f32[72,128]{1,0:T(8,128)S(1)} %get-tuple-element.15), channel_id=1, source_target_pairs={{0,16},{32,48},{64,80},{96,112},{128,144},{160,176},{192,208},{224... | collective-permute-start | bytes 110600 | tf_op jit(solution)/shard_map/ppermute | solution.py:472
  9.0 1.7 %collective-permute-start.1 = (f32[72,128]{1,0:T(8,128)S(1)}, f32[72,128]{1,0:T(8,128)S(1)}, u32[]{:S(2)}, u32[]{:S(2)}) collective-permute-start(f32[72,128]{1,0:T(8,128)S(1)} %get-tuple-element.16), channel_id=1, source_target_pairs={{16,32},{48,64},{80,96},{112,128},{144,160},{176,192},{208,224},{3... | collective-permute-start | bytes 110600 | tf_op jit(solution)/shard_map/ppermute | solution.py:472
  9.7 1.9 %copy-start.1 = (f32[4,32,16,4]{1,3,2,0:T(4,128)S(1)}, f32[4,32,16,4]{1,3,2,0:T(4,128)}, u32[]{:S(2)}) copy-start(f32[4,32,16,4]{1,3,2,0:T(4,128)} %param.4) | copy-start | bytes 98308
  9.7 1.9 %copy-start.2 = (f32[4]{0:T(128)S(1)}, f32[4]{0:T(128)}, u32[]{:S(2)}) copy-start(f32[4]{0:T(128)} %nominal_weights.1) | copy-start | bytes 52
  18.5 1.8 %collective-permute-start.4 = (f32[768,128]{1,0:T(8,128)S(1)}, f32[768,128]{1,0:T(8,128)S(1)}, u32[]{:S(2)}, u32[]{:S(2)}) collective-permute-start(f32[768,128]{1,0:T(8,128)S(1)} %get-tuple-element.20), channel_id=1, source_target_pairs={{0,1},{1,0},{2,3},{3,2},{4,5},{5,4},{6,7},{7,6},{8,9},{9,8},{10,11... | collective-permute-start | bytes 1179656 | tf_op jit(solution)/shard_map/ppermute | solution.py:512
  39.5 2.9 %collective-permute-start.5 = (f32[48,128]{1,0:T(8,128)S(1)}, f32[48,128]{1,0:T(8,128)S(1)}, u32[]{:S(2)}, u32[]{:S(2)}) collective-permute-start(f32[48,128]{1,0:T(8,128)S(1)} %reduce_sum.9), channel_id=1, source_target_pairs={{0,2},{1,3},{2,0},{3,1},{4,6},{5,7},{6,4},{7,5},{8,10},{9,11},{10,... | collective-permute-start | bytes 73736 | tf_op jit(solution)/shard_map/ppermute | solution.py:423
  42.4 5.4 %collective-permute-start.6 = (f32[48,128]{1,0:T(8,128)S(1)}, f32[48,128]{1,0:T(8,128)S(1)}, u32[]{:S(2)}, u32[]{:S(2)}) collective-permute-start(f32[48,128]{1,0:T(8,128)S(1)} %add.22), channel_id=1, source_target_pairs={{0,4},{1,5},{2,6},{3,7},{4,0},{5,1},{6,2},{7,3},{8,12},{9,13},{10,... | collective-permute-start | bytes 73736 | tf_op jit(solution)/shard_map/ppermute | solution.py:423
  47.9 6.6 %collective-permute-start.7 = (f32[48,128]{1,0:T(8,128)S(1)}, f32[48,128]{1,0:T(8,128)S(1)}, u32[]{:S(2)}, u32[]{:S(2)}) collective-permute-start(f32[48,128]{1,0:T(8,128)S(1)} %add.23), channel_id=1, source_target_pairs={{0,8},{1,9},{2,10},{3,11},{4,12},{5,13},{6,14},{7,15},{8,0},{9,1},... | collective-permute-start | bytes 73736 | tf_op jit(solution)/shard_map/ppermute | solution.py:423
  66.0 10.2 %collective-permute-start.8 = (f32[768,128]{1,0:T(8,128)S(1)}, f32[768,128]{1,0:T(8,128)S(1)}, u32[]{:S(2)}, u32[]{:S(2)}) collective-permute-start(f32[768,128]{1,0:T(8,128)S(1)} %bitcast.16), channel_id=1, source_target_pairs={{0,1},{1,0},{2,3},{3,2},{4,5},{5,4},{6,7},{7,6},{8,9},{9,8},{10,11... | collective-permute-start | bytes 1179656 | tf_op jit(solution)/shard_map/ppermute | solution.py:514
